TPU v7x, 128 devices: a whole 4x4x4 slice. The times are simulated.
128 devices in a mesh: circ: 8 (over z, y_lo), mer: 16 (over x, y_hi, core).
Axes of the slice: x: 4, y: 4 (y_hi: 2, y_lo: 2; y = y_hi * 2 + y_lo), z: 4, core: 2. Of those that a mesh axis runs over, the one named last changes fastest.
Arguments:
- adjoint: float32 [6, 16, 4096], P(None, 'circ', 'mer'), may hold values from -6 to 6
- mode_fields: float32 [3, 6, 16, 4096], P(None, None, 'circ'), may hold values from -6 to 6
- node_slot: int32 [4096], replicated, may hold values from 0 to 4095, as said below
- thickness: float32 [16, 4096], P('circ'), may hold values from 0.5 to 1.5
- weld_land: int32 [16, 4096], P('circ'), may hold values 0 or 1
- panel_spans: int32 [8, 16], P('circ'), may hold values from 1 to 768, 4096 in all within a row
- load_factor: float32 [], replicated, may hold values from 0.5 to 1.5
- membrane: float32 [24, 24], replicated, may hold values from -1.25 to 1.25
- bending: float32 [24, 24], replicated, may hold values from -0.4375 to 0.4375
- geometric: float32 [3, 24, 24], replicated, may hold values from -1.25 to 1.25
- stress_map: float32 [3, 24], replicated, may hold values from -1.25 to 1.25
Outputs:
- adjoint_load: float32 [6, 16, 4096], P(None, 'circ', 'mer')
- thickness_grad: float32 [16, 12288], P('circ', 'mer')
Inputs may be any that keep to these rules, and one draw needn't show every extreme that they name: A permutation of the node positions; node_slot[j] // 256 equals j modulo 4096 // 256. `panel_spans`: each row sums to 4096 and its largest entry is 768.
All inputs are finite; a program needn't handle non-finite values. No bound on the sum of `weld_land` on one device may be relied on, other than what follows from the above.
Results may differ from a plain program's by a relative error of at most 0.0003.
Values sent between devices are 32-bit elements; how exact they have to be, the bound alone decides.
No kernel may reach another device: no remote copies, remote signals or barrier semaphores. Data moves between devices by JAX's collectives and lax.ppermute only.
A program may use at most 128 MiB of HBM per device.

v0:
```python
import jax
import jax.numpy as jnp
from jax import lax
from jax.sharding import PartitionSpec as P

MOST = 768


highest = lax.Precision.HIGHEST


def from_behind(block, axis, distance):
    devices = range(lax.axis_size(axis))
    route = [((i - distance) % len(devices), i) for i in devices]
    return lax.ppermute(block, axis, route)


def element_terms(
    mode_vectors,
    adjoint_vectors,
    thick_rows,
    weld_rows,
    load_factor,
    membrane,
    bending,
    geometric,
    stress_map,
):
    land_growth = 1.0 + 0.5 * weld_rows
    thick_eff = thick_rows * land_growth
    membrane_part = jnp.einsum("ab,fbe->fae", membrane, mode_vectors, precision=highest)
    bending_part = jnp.einsum("ab,fbe->fae", bending, mode_vectors, precision=highest)
    tangent = membrane_part + 3.0 * thick_eff**2 * bending_part
    stiffness = jnp.sum(mode_vectors[0] * tangent[0] + mode_vectors[1] * tangent[1], axis=0)
    adjoint_term = jnp.sum(adjoint_vectors * tangent[2], axis=0)
    stress = jnp.dot(stress_map, mode_vectors[2], precision=highest)
    geometric_part = jnp.einsum("sab,kbe->ksae", geometric, mode_vectors[:2], precision=highest)
    pair_terms = jnp.sum(mode_vectors[:2, None] * geometric_part, axis=(0, 2))
    gradient = land_growth * (
        stiffness - load_factor * jnp.sum(stress * pair_terms, axis=0) - adjoint_term
    )
    load_rows = load_factor * thick_eff * jnp.dot(stress_map.T, pair_terms, precision=highest)
    return (gradient, load_rows)


def corner_values(field, upper_rim, cols_here, cols_next):
    lower_here = jnp.take(field, cols_here, axis=-1)
    lower_next = jnp.take(field, cols_next, axis=-1)
    rim_here = jnp.take(upper_rim, cols_here, axis=-1)
    rim_next = jnp.take(upper_rim, cols_next, axis=-1)
    upper_here = jnp.concatenate([lower_here[..., 1:, :], rim_here], axis=-2)
    upper_next = jnp.concatenate([lower_next[..., 1:, :], rim_next], axis=-2)
    return jnp.stack([lower_here, upper_here, upper_next, lower_next], axis=-4)


def on_device(
    adjoint,
    mode_fields,
    node_slot,
    thickness,
    weld_land,
    panel_spans,
    load_factor,
    membrane,
    bending,
    geometric,
    stress_map,
):
    cycle_count = adjoint.shape[1]
    owned_width = adjoint.shape[2]
    column_width = mode_fields.shape[3]
    block_width = min(128, owned_width)
    elements = cycle_count * block_width
    member = lax.axis_index("mer")
    group_size = lax.axis_size("mer")
    spans_row = panel_spans[0]
    span_count = spans_row[member]
    span_start = jnp.sum(jnp.where(jnp.arange(group_size, dtype=jnp.int32) < member, spans_row, 0))
    adj_column = lax.all_gather(adjoint, "mer", axis=2, tiled=True)
    adj_rim, mode_rim = from_behind((adj_column[:, :1], mode_fields[:, :, :1]), "circ", -1)
    cycle_ids = jnp.arange(cycle_count, dtype=jnp.int32)[:, None]

    def block_terms(accumulated, meridional, validity):
        cols_here = jnp.take(node_slot, meridional)
        cols_next = jnp.take(node_slot, (meridional + 1) % column_width)
        mode_vectors = corner_values(mode_fields, mode_rim, cols_here, cols_next).reshape(
            3, 24, elements
        )
        adjoint_vectors = corner_values(adj_column, adj_rim, cols_here, cols_next).reshape(
            24, elements
        )
        thick_rows = jnp.take(thickness, meridional, axis=1).reshape(elements)
        weld_rows = jnp.take(weld_land, meridional, axis=1).reshape(elements).astype(jnp.float32)
        gradient, load_rows = element_terms(
            mode_vectors,
            adjoint_vectors,
            thick_rows,
            weld_rows,
            load_factor,
            membrane,
            bending,
            geometric,
            stress_map,
        )
        load_rows = load_rows.reshape(4, 6, cycle_count, block_width) * validity
        accumulated = accumulated.at[:, cycle_ids, cols_here[None, :]].add(load_rows[0])
        accumulated = accumulated.at[:, cycle_ids + 1, cols_here[None, :]].add(load_rows[1])
        accumulated = accumulated.at[:, cycle_ids + 1, cols_next[None, :]].add(load_rows[2])
        accumulated = accumulated.at[:, cycle_ids, cols_next[None, :]].add(load_rows[3])
        return (accumulated, gradient.reshape(cycle_count, block_width) * validity)

    zero_loads = jnp.zeros((6, cycle_count + 1, column_width), jnp.float32)
    positions = jnp.arange(block_width, dtype=jnp.int32)

    def visit_owned(block_index, carry):
        accumulated, gradients = carry
        offset = block_index * block_width + positions
        validity = (offset < span_count).astype(jnp.float32)
        accumulated, gradient = block_terms(
            accumulated, (span_start + offset) % column_width, validity
        )
        gradients = lax.dynamic_update_slice_in_dim(
            gradients, gradient, block_index * block_width, 1
        )
        return (accumulated, gradients)

    block_total = (span_count + block_width - 1) // block_width
    accumulated, thickness_grad = lax.fori_loop(
        0, block_total, visit_owned, (zero_loads, jnp.zeros((cycle_count, MOST), jnp.float32))
    )
    reduced = lax.psum_scatter(accumulated, "mer", scatter_dimension=2, tiled=True)
    carried = from_behind(reduced[:, cycle_count:], "circ", 1)
    adjoint_load = reduced[:, :cycle_count].at[:, :1].add(carried)
    return (adjoint_load, thickness_grad)


def solution(mesh):
    return jax.shard_map(
        on_device,
        mesh=mesh,
        in_specs=(
            P(None, "circ", "mer"),
            P(None, None, "circ", None),
            P(),
            P("circ", None),
            P("circ", None),
            P("circ", None),
            P(),
            P(),
            P(),
            P(),
            P(),
        ),
        out_specs=(P(None, "circ", "mer"), P("circ", "mer")),
        check_vma=False,
    )
```

profile of v0, /device:TPU:1, one launch (start us, length us, event | category | flops | bytes accessed | tf_op | source)
XLA Modules:
  0.0 1076.2 jit_solution(930832853254150709)
XLA Ops:
  7.2 1.3 slice.132
  8.5 5.7 collective-permute-start
  14.1 25.6 %all_gather.3 = f32[6,2,4096]{2,1,0:T(2,128)S(1)} all-gather(f32[6,2,256]{2,1,0:T(2,128)} %param.25), channel_id=1, replica_groups=mesh['circ'=8,'mer'=16] {'mer'}, dimensions={2}, use_global_device_ids=true | all-gather | bytes 208896 | tf_op jit(solution)/shard_map/all_gather | solution.py:79
  39.9 1.2 constant_dynamic-slice_fusion
  41.8 4.5 copy.269
  46.2 14.1 %copy.267 = f32[3,6,2,4096]{1,2,3,0:T(2,128)} copy(f32[3,6,2,4096]{3,2,1,0:T(2,128)} %param.26) | data formatting | bytes 1179648
  60.3 2.0 copy.265
  62.3 2.0 copy.266
  64.3 0.7 fusion.38
  65.0 0.7 copy.270
  65.7 5.9 copy.268
  71.6 3.1 broadcast_in_dim.128
  74.7 147.8 %while.17 = (s32[]{:T(128)}, f32[6,3,4096]{0,2,1:T(8,128)}, f32[2,768]{1,0:T(2,128)S(1)}, s32[]{:T(128)}, s32[]{:T(128)}, /*index=5*/s32[4096]{0:T(1024)S(1)}, f...) while((s32[]{:T(128)}, f32[6,3,4096]{0,2,1:T(8,128)}, ...), condition=%wide.region_10.16_spmd.clone.clone, body=%wide.region_1.15_spmd.clone.clone.sunk | while | flops 21983908 | bytes 2950539 | solution.py:128
  74.9 1.3 compare_and_fusion.5
  76.2 1.1 gather_fusion.1
  77.4 5.7 gather_fusion.5
  83.4 4.1 gather_fusion.4
  87.7 0.7 compare_select_fusion.17
  88.4 1.1 gather_fusion
  89.5 0.7 clamp_shift-left_fusion.5
  90.2 5.7 gather_fusion.2
  96.2 4.1 gather_fusion.3
  101.0 0.6 fusion.89
  101.6 2.2 gather_fusion.6
  103.9 2.3 gather_fusion.7
  106.2 0.7 multiply_bitcast_fusion.3
  107.1 2.9 gather_fusion.11
  110.4 0.6 gather_fusion.10
  111.4 2.9 gather_fusion.8
  114.6 0.6 gather_fusion.9
  115.6 0.3 pad_maximum_fusion.11
  116.4 0.3 fusion.88
  116.9 0.7 fusion.98
  118.1 26.0 %scatter_fusion = f32[6,3,4096]{0,2,1:T(8,128)} fusion(f32[6,3,4096]{0,2,1:T(8,128)} %get-tuple-element.811, s32[256]{0:T(256)S(1)} %get-tuple-element.765, f32[256,6]{1,0:T(8,128)S(1)} %bitcast.246), kind=kCustom, calls=%fused_computation.12.clone.clone.1 | custom fusion | flops 1536 | bytes 20480 | tf_op jit(solution)/shard_map/while/body/scatter-add | solution.py:106
  144.2 25.9 %scatter_fusion.1 = f32[6,3,4096]{0,2,1:T(8,128)} fusion(f32[6,3,4096]{0,2,1:T(8,128)} %scatter_fusion, s32[256]{0:T(256)S(1)} %get-tuple-element.772, f32[256,6]{1,0:T(8,128)S(1)} %bitcast.248), kind=kCustom, calls=%fused_computation.13.clone.clone.1 | custom fusion | flops 1536 | bytes 20480 | tf_op jit(solution)/shard_map/while/body/scatter-add | solution.py:107
  170.3 26.0 %scatter_fusion.2 = f32[6,3,4096]{0,2,1:T(8,128)} fusion(f32[6,3,4096]{0,2,1:T(8,128)} %scatter_fusion.1, s32[256]{0:T(256)S(1)} %get-tuple-element.774, f32[256,6]{1,0:T(8,128)S(1)} %bitcast.249), kind=kCustom, calls=%fused_computation.14.clone.clone.1 | custom fusion | flops 1536 | bytes 20480 | tf_op jit(solution)/shard_map/while/body/scatter-add | solution.py:108
  196.5 26.0 %scatter_fusion.3 = f32[6,3,4096]{0,2,1:T(8,128)} fusion(f32[6,3,4096]{0,2,1:T(8,128)} %scatter_fusion.2, s32[256]{0:T(256)S(1)} %get-tuple-element.776, f32[256,6]{1,0:T(8,128)S(1)} %bitcast.247), kind=kCustom, calls=%fused_computation.15.clone.clone.1 | custom fusion | flops 1536 | bytes 20480 | tf_op jit(solution)/shard_map/while/body/scatter-add | solution.py:109
  222.5 27.6 %copy.277 = f32[6,3,4096]{1,0,2:T(8,128)} copy(f32[6,3,4096]{0,2,1:T(8,128)} %get-tuple-element.279) | data formatting | bytes 589824
  250.1 10.9 %reshape.562 = f32[4096,18]{1,0:T(8,128)} reshape(f32[4096,6,3]{2,1,0:T(8,128)} %bitcast.239) | data formatting | bytes 589824
  261.0 801.3 %reduce-scatter.4.cloned.1.call-done = f32[256,18]{1,0:T(8,128)} async-done(((f32[4096,18]{1,0:T(8,128)}), f32[256,18]{1,0:T(8,128)}) %reduce-scatter.4.cloned.1.call-update) | async-done | bytes 18448
  1062.3 1.1 reshape.563
  1063.4 0.3 fusion.41
  1063.8 0.3 copy.282
  1064.1 0.5 collective-permute-start.2
  1064.6 0.3 copy.281
  1064.9 0.3 copy.280
  1065.2 3.5 collective-permute-done.2
  1068.8 0.6 copy-done.7
  (89 shorter events, 4.6 us)
Async XLA Ops:
  7.2 1055.1 %reduce-scatter.4.cloned.1.call-start = ((), (), s32[]{:S(2)}) async-start(), calls=%async_computation.1 | async-start | bytes 2228224
  8.5 57.2 %collective-permute-start = (f32[3,6,1,4096]{3,2,1,0:T(1,128)S(1)}, f32[3,6,1,4096]{3,2,1,0:T(1,128)S(1)}, u32[]{:S(2)}, u32[]{:S(2)}) collective-permute-start(f32[3,6,1,4096]{3,2,1,0:T(1,128)S(1)} %slice.132), channel_id=1, source_target_pairs={{16,0},{32,16},{48,32},{64,48},{80,64},{96,80},{112,96},{0,112},{1... | collective-permute-start | bytes 884744 | tf_op jit(solution)/shard_map/ppermute | solution.py:15
  39.8 25.2 %collective-permute-start.1 = (f32[6,1,4096]{2,1,0:T(1,128)S(1)}, f32[6,1,4096]{2,1,0:T(1,128)S(1)}, u32[]{:S(2)}, u32[]{:S(2)}) collective-permute-start(f32[6,1,4096]{2,1,0:T(1,128)S(1)} %slice.214), channel_id=1, source_target_pairs={{16,0},{32,16},{48,32},{64,48},{80,64},{96,80},{112,96},{0,112},{1... | collective-permute-start | bytes 294920 | tf_op jit(solution)/shard_map/ppermute | solution.py:15
  46.2 14.1 %copy-start.5 = (f32[2,4096]{1,0:T(2,128)S(1)}, f32[2,4096]{1,0:T(2,128)}, u32[]{:S(2)}) copy-start(f32[2,4096]{1,0:T(2,128)} %param.28) | copy-start | bytes 98308
  46.2 16.1 %copy-start.6 = (s32[2,4096]{1,0:T(2,128)S(1)}, s32[2,4096]{1,0:T(2,128)}, u32[]{:S(2)}) copy-start(s32[2,4096]{1,0:T(2,128)} %param.29) | copy-start | bytes 98308
  46.2 18.1 %copy-start.9 = (s32[1,16]{1,0:T(1,128)S(1)}, s32[1,16]{1,0:T(1,128)}, u32[]{:S(2)}) copy-start(s32[1,16]{1,0:T(1,128)} %param.30) | copy-start | bytes 196
  65.6 9.1 copy-start
  65.6 9.1 copy-start.1
  65.7 9.1 copy-start.2
  65.7 9.1 copy-start.3
  65.7 9.1 copy-start.4
  222.5 27.6 %copy-start.8 = (f32[2,768]{1,0:T(2,128)}, f32[2,768]{1,0:T(2,128)S(1)}, u32[]{:S(2)}) copy-start(f32[2,768]{1,0:T(2,128)S(1)} %get-tuple-element.507) | copy-start | bytes 18436
  1064.1 4.6 collective-permute-start.2
  1068.8 0.6 copy-start.7
Sparse Core Ops, SparseCore 0:
  261.1 801.1 reduce-scatter.3
where the time goes:
time: 1100 us; the launch traced here: 1080 us
  waiting for transfers between devices  805 us (73%)
  local copies, waits for them, and re-layouts  112 us (10%)
  other arithmetic  111 us (10%)
  blocking collectives  25.6 us (2%)
  between operations  14.8 us (1%)
    unnamed x2, waiting for transfers between devices  801 us
    unnamed x32, local copies, waits for them, and re-layouts  70.3 us
    scatter-add x1, other arithmetic, block_terms(): accumulated.at[:, cycle_ids, cols_here[None, :]].add(load_rows[0])  26 us
    scatter-add x1, other arithmetic, block_terms(): accumulated.at[:, cycle_ids + 1, cols_next[None, :]].add(load_rows[2])  26 us
    scatter-add x1, other arithmetic, block_terms(): accumulated.at[:, cycle_ids, cols_next[None, :]].add(load_rows[3])  26 us
    scatter-add x1, other arithmetic, block_terms(): accumulated.at[:, cycle_ids + 1, cols_here[None, :]].add(load_rows[1])  25.9 us
    all_gather x1, blocking collectives, on_device(): adj_column = lax.all_gather(adjoint, 'mer', axis=2, tiled=True)  25.6 us
  transfers between devices with their start and end apart: 4, of which 2 were waited for; matrix products, arithmetic and copies ran while one was open for 2% of the time, Pallas kernels for 0%

commit v1 on v0

v1 whole, which is shorter than its diff:
```python
import jax
import jax.numpy as jnp
from jax import lax
from jax.experimental import pallas as pl
from jax.experimental.pallas import tpu as pltpu
from jax.sharding import PartitionSpec as P

DOF = 6
PAD = 8
OWN = 256
GROUPS = 16
COLUMN = OWN * GROUPS
MOST = 768
LANES = 128
ROWS = COLUMN // LANES
WINDOW = 128
SPREAD = 1024

f32, bf16, i32 = jnp.float32, jnp.bfloat16, jnp.int32
vmem = pl.BlockSpec(memory_space=pltpu.VMEM)
smem = pl.BlockSpec(memory_space=pltpu.SMEM)
raw = pl.BlockSpec(memory_space=pl.ANY)


def iota(shape, axis):
    return lax.broadcasted_iota(i32, shape, axis)


def parts(x):
    high = x.astype(bf16)
    rest = x - high.astype(f32)
    middle = rest.astype(bf16)
    low = (rest - middle.astype(f32)).astype(bf16)
    return high, middle, low


def matmul(a, b):
    return jnp.dot(a, b, preferred_element_type=f32)


def matmul_nt(a, b):
    return lax.dot_general(a, b, (((1,), (1,)), ((), ())), preferred_element_type=f32)


def left_stack(three, axis):
    high, middle, low = three
    return jnp.concatenate([high, high, middle, middle, high, low], axis=axis)


def right_stack(three, axis):
    high, middle, low = three
    return jnp.concatenate([high, middle, high, middle, low, high], axis=axis)


def gather_kernel(modes, adjoint, own, own_adjoint, rim, held, sems):
    member = lax.axis_index("mer")
    copies = []
    for d in range(3):
        block = (member + (d + GROUPS - 1)) & (GROUPS - 1)
        columns = pl.ds(pl.multiple_of(block * OWN, OWN), OWN)
        copies.append(pltpu.make_async_copy(modes.at[:, :, :, columns], held.at[d], sems.at[d]))
        copies[-1].start()
    own[...] = jnp.zeros_like(own)
    own_adjoint[...] = jnp.zeros_like(own_adjoint)
    rim[...] = jnp.zeros_like(rim)
    for i in range(DOF):
        pair = adjoint[i]
        rim[9 * PAD + i : 9 * PAD + i + 1, :] = pair[0:1]
        own_adjoint[i : i + 1, :] = pair[0:1]
        own_adjoint[PAD + i : PAD + i + 1, :] = pair[1:2]
    for d in range(3):
        copies[d].wait()
        for f in range(3):
            for i in range(DOF):
                pair = held[d, f, i]
                rim[(3 * d + f) * PAD + i : (3 * d + f) * PAD + i + 1, :] = pair[0:1]
                own[d, f * PAD + i : f * PAD + i + 1, :] = pair[0:1]
                own[d, (3 + f) * PAD + i : (3 + f) * PAD + i + 1, :] = pair[1:2]


def element_kernel(
    own,
    own_adjoint,
    rim,
    slots,
    thickness,
    weld,
    spans,
    factor,
    membrane,
    bending,
    geometric,
    stress_map,
    sent,
    loads,
    carry,
    thick_rows,
    weld_rows,
    nodes,
):
    member = lax.axis_index("mer")
    load_factor = factor[0]

    lane = iota((1, OWN), 1)
    position = [(lane * GROUPS + (member + d - 1)) & (COLUMN - 1) for d in range(3)]
    pick = [
        (iota((LANES, OWN), 0) == (position[d] & (LANES - 1))).astype(f32).astype(bf16)
        for d in range(3)
    ]
    for a in range(ROWS):
        thick_rows[2 * a : 2 * a + 2, :] = thickness[:, a * LANES : (a + 1) * LANES]
        weld_rows[2 * a : 2 * a + 2, :] = weld[:, a * LANES : (a + 1) * LANES]
    thick_parts = parts(thick_rows[...])
    weld_part = weld_rows[...].astype(f32).astype(bf16)
    slot_part = (slots[...] & (OWN - 1)).astype(f32).astype(bf16)

    def choose(rows, d, stride, offset):
        return jnp.sum(
            jnp.where(
                iota(rows.shape, 0) == (position[d] >> 7) * stride + offset,
                rows,
                0.0,
            ),
            axis=0,
            keepdims=True,
        )

    growth, thick = {}, {}
    stacked = jnp.concatenate([*thick_parts, weld_part], axis=0)
    for d in range(2):
        rows = matmul(stacked, pick[d])
        thick_all = (rows[0:64] + rows[64:128]) + rows[128:192]
        for r in range(2):
            growth[d, r] = 1.0 + 0.5 * choose(rows[192:256], d, 2, r)
            thick[d, r] = choose(thick_all, d, 2, r) * growth[d, r]
    order = []
    for d in range(3):
        slot = choose(matmul(slot_part, pick[d]), d, 1, 0).astype(i32)
        order.append((iota((OWN, OWN), 0) == slot).astype(f32).astype(bf16))

    for d in range(3):
        pieces = [own[d], rim[3 * d * PAD : 3 * (d + 1) * PAD, :]]
        if d == 1:
            pieces += [own_adjoint[...], rim[9 * PAD : 10 * PAD, :]]
        values = jnp.concatenate(pieces, axis=0)
        count = values.shape[0]
        placed = matmul(jnp.concatenate(parts(values), axis=0), order[d])
        for p in range(3):
            nodes[d, p, 0:count, :] = placed[p * count : (p + 1) * count]

    spread = (
        iota((24, 32), 1) == (iota((24, 32), 0) // 6) * PAD + iota((24, 32), 0) % 6
    ).astype(f32).astype(bf16)
    spread_t = (
        iota((32, 24), 0) == (iota((32, 24), 1) // 6) * PAD + iota((32, 24), 1) % 6
    ).astype(f32).astype(bf16)
    stress_rows = jnp.concatenate([stress_map[...], jnp.zeros((5, 24), f32)], axis=0)
    matrices = [membrane[...], bending[...], geometric[0], geometric[1], geometric[2]]
    weights = [[], [], []]
    for matrix in matrices:
        for p, part in enumerate(parts(matrix)):
            wide = matmul(part, spread).astype(bf16)
            weights[p].append(matmul(spread_t, wide))
    stress_parts = parts(stress_rows)
    for p, part in enumerate(stress_parts):
        weights[p].append(matmul(part, spread))
        weights[p].append(jnp.zeros((PAD, 32), f32))
    weights = left_stack([jnp.concatenate(w, axis=0).astype(bf16) for w in weights], 1)
    load_weights = left_stack([matmul_nt(spread_t, part).astype(bf16) for part in stress_parts], 1)
    pair_weights = weights[64:160]
    prestate_weights = jnp.concatenate([weights[0:64], weights[160:176]], axis=0)

    def corner_parts(f, d, r):
        low, high = (f + 3 * r) * PAD, (f + 3 * (r + 1)) * PAD
        out = []
        for p in range(3):
            out.append(
                jnp.concatenate(
                    [
                        nodes[d, p, low : low + PAD, :],
                        nodes[d, p, high : high + PAD, :],
                        nodes[d + 1, p, high : high + PAD, :],
                        nodes[d + 1, p, low : low + PAD, :],
                    ],
                    axis=0,
                )
            )
        return out

    def fold(x):
        return (x[0:8] + x[8:16]) + (x[16:24] + x[24:32])

    def column_sum(x):
        return jnp.sum(x, axis=0, keepdims=True)

    adjoint = [
        (nodes[1, 0, g : g + PAD, :] + nodes[1, 1, g : g + PAD, :]) + nodes[1, 2, g : g + PAD, :]
        for g in (72, 80, 88)
    ]
    result = []
    delayed = []
    load_tiles = {}
    for r in range(2):
        for d in (1, 0):
            bend = 3.0 * thick[d, r] * thick[d, r]
            stiff = jnp.zeros((PAD, OWN), f32)
            pairs = [jnp.zeros((PAD, OWN), f32)] * 3
            for f in range(2):
                three = corner_parts(f, d, r)
                value = (three[0] + three[1]) + three[2]
                stack = right_stack([t.astype(bf16) for t in three], 0)
                if d == 1:
                    product = matmul(weights[0:160], stack)
                    stiff = stiff + fold(value * (product[0:32] + bend * product[32:64]))
                    product = product[64:160]
                else:
                    product = matmul(pair_weights, stack)
                pairs = [
                    pairs[s] + fold(value * product[32 * s : 32 * s + 32]) for s in range(3)
                ]
            pairs = [column_sum(x) for x in pairs]
            three = corner_parts(2, d, r)
            product = matmul(prestate_weights, right_stack([t.astype(bf16) for t in three], 0))
            tangent = product[0:32] + bend * product[32:64]
            if d == 1:
                aterm = column_sum(adjoint[r] * tangent[0:8] + adjoint[r + 1] * tangent[8:16])
                coupling = (
                    product[64:65] * pairs[0] + product[65:66] * pairs[1]
                ) + product[66:67] * pairs[2]
                result.append(
                    growth[d, r] * (column_sum(stiff) - load_factor * coupling - aterm)
                )
            else:
                aterm = column_sum(adjoint[r] * tangent[24:32] + adjoint[r + 1] * tangent[16:24])
                delayed.append(-(growth[d, r] * aterm))
            scale = load_factor * thick[d, r]
            scaled = jnp.concatenate(
                [scale * x for x in pairs] + [jnp.zeros((5, OWN), f32)], axis=0
            )
            load_tiles[d, r] = matmul(load_weights, right_stack(parts(scaled), 0))

    here = [
        load_tiles[1, 0][0:8] + load_tiles[0, 0][24:32],
        (load_tiles[1, 1][0:8] + load_tiles[0, 1][24:32])
        + (load_tiles[1, 0][8:16] + load_tiles[0, 0][16:24]),
        load_tiles[1, 1][8:16] + load_tiles[0, 1][16:24],
    ]
    stored = matmul_nt(jnp.concatenate(parts(jnp.concatenate(here, axis=0)), axis=0), order[1])
    stored = (stored[0:24] + stored[24:48]) + stored[48:72]
    loads[...] = stored[0:16]
    carry[...] = stored[16:24]

    outgoing = jnp.concatenate(result + delayed + [jnp.zeros((4, OWN), f32)], axis=0)
    start = jnp.int32(0)
    for target in range(GROUPS):
        first = (start >> 4) & (OWN - 1)
        turned = pltpu.roll(outgoing, (OWN - first) & (OWN - 1), 1)
        sent[target] = turned[:, 0:WINDOW]
        start = start + spans[0, target]


def span_kernel(received, loads, carry, spans, adjoint_load, thickness_grad):
    member = lax.axis_index("mer")
    start = jnp.int32(0)
    for target in range(GROUPS):
        start = start + jnp.where(target < member, spans[0, target], 0)
    count = spans[0, member]
    offset = start & (GROUPS - 1)

    values = received[...].reshape(GROUPS * PAD, WINDOW)
    expand = (iota((WINDOW, SPREAD), 0) == (iota((WINDOW, SPREAD), 1) >> 4)).astype(f32).astype(bf16)
    rows = matmul(jnp.concatenate(parts(values), axis=0), expand)
    n = GROUPS * PAD
    rows = (rows[0:n] + rows[n : 2 * n]) + rows[2 * n : 3 * n]
    residue = iota((PAD, SPREAD), 1) & (GROUPS - 1)
    sequence = jnp.zeros((PAD, SPREAD), f32)
    for g in range(GROUPS):
        sequence = jnp.where(residue == g, rows[g * PAD : (g + 1) * PAD], sequence)
    now = pltpu.roll(sequence, (SPREAD - offset) & (SPREAD - 1), 1)
    late = pltpu.roll(sequence, (SPREAD - 1 - offset) & (SPREAD - 1), 1)
    gradient = now[0:2, 0:MOST] + late[2:4, 0:MOST]
    thickness_grad[...] = jnp.where(iota((2, MOST), 1) < count, gradient, 0.0)

    first = loads[0:PAD] + carry[...]
    second = loads[PAD : 2 * PAD]
    for i in range(DOF):
        adjoint_load[i, 0:1, :] = first[i : i + 1]
        adjoint_load[i, 1:2, :] = second[i : i + 1]


def shape(*dims):
    return jax.ShapeDtypeStruct(dims, f32)


def from_behind(block, axis, distance):
    size = lax.axis_size(axis)
    return lax.ppermute(block, axis, [((i - distance) % size, i) for i in range(size)])


def on_device(
    adjoint,
    mode_fields,
    node_slot,
    thickness,
    weld_land,
    panel_spans,
    load_factor,
    membrane,
    bending,
    geometric,
    stress_map,
):
    own, own_adjoint, rim = pl.pallas_call(
        gather_kernel,
        out_shape=(shape(3, 6 * PAD, OWN), shape(2 * PAD, OWN), shape(10 * PAD, OWN)),
        in_specs=[raw, vmem],
        out_specs=(vmem, vmem, vmem),
        scratch_shapes=[pltpu.VMEM((3, 3, DOF, 2, OWN), f32), pltpu.SemaphoreType.DMA((3,))],
    )(mode_fields, adjoint)
    rim = from_behind(rim, "circ", -1)
    sent, loads, carry = pl.pallas_call(
        element_kernel,
        out_shape=(shape(GROUPS, PAD, WINDOW), shape(2 * PAD, OWN), shape(PAD, OWN)),
        in_specs=[vmem] * 6 + [smem, smem] + [vmem] * 4,
        out_specs=(vmem, vmem, vmem),
        scratch_shapes=[
            pltpu.VMEM((2 * ROWS, LANES), f32),
            pltpu.VMEM((2 * ROWS, LANES), i32),
            pltpu.VMEM((3, 3, 12 * PAD, OWN), f32),
        ],
    )(
        own,
        own_adjoint,
        rim,
        node_slot.reshape(ROWS, LANES),
        thickness,
        weld_land,
        panel_spans,
        load_factor.reshape(1),
        membrane,
        bending,
        geometric,
        stress_map,
    )
    carry = from_behind(carry, "circ", 1)
    received = lax.all_to_all(sent, "mer", 0, 0)
    return pl.pallas_call(
        span_kernel,
        out_shape=(shape(DOF, 2, OWN), shape(2, MOST)),
        in_specs=[vmem] * 3 + [smem],
        out_specs=(vmem, vmem),
    )(received, loads, carry, panel_spans)


def solution(mesh):
    return jax.shard_map(
        on_device,
        mesh=mesh,
        in_specs=(
            P(None, "circ", "mer"),
            P(None, None, "circ", None),
            P(),
            P("circ", None),
            P("circ", None),
            P("circ", None),
            P(),
            P(),
            P(),
            P(),
            P(),
        ),
        out_specs=(P(None, "circ", "mer"), P("circ", "mer")),
        check_vma=False,
    )
```

time: 1100 us -> 33.4 us (0.03); the launches traced: 1080 us -> 33 us
  waiting for transfers between devices: 805 us -> 8.43 us
  other arithmetic: 111 us -> 0 us
  local copies, waits for them, and re-layouts: 112 us -> 1.27 us
  blocking collectives: 25.6 us -> 0 us
  between operations: 14.8 us -> 1.31 us
    unnamed x2 -> x0, waiting for transfers between devices: 801 us -> none
    scatter-add x4 -> x0, other arithmetic: 104 us -> none  [the longest x1 26 us: block_terms(): accumulated.at[:, cycle_ids, cols_here[None, :]].add(load_rows[0])]
    unnamed x32 -> x8, local copies, waits for them, and re-layouts: 70.3 us -> 1.27 us
    gather x18 -> x0, local copies, waits for them, and re-layouts: 34.4 us -> none  [the longest x3 8.87 us: corner_values(): lower_here = jnp.take(field, cols_here, axis=-1)]
    all_gather x1 -> x0, blocking collectives: 25.6 us -> none  [on_device(): adj_column = lax.all_gather(adjoint, 'mer', axis=2, tiled=True)]
  transfers between devices with their start and end apart: 4 -> 3, of which waited for: 2 -> 3; matrix products, arithmetic and copies ran while one was open for 2% -> 0% of each run, Pallas kernels for 0% -> 0%
where the time goes in v1:
time: 33.4 us; the launch traced here: 33 us
  starting transfers between devices  14 us (42%)
  waiting for transfers between devices  8.43 us (25%)
  Pallas kernels  7.97 us (24%)
  between operations  1.31 us (4%)
  local copies, waits for them, and re-layouts  1.27 us (4%)
    all_to_all x1, starting transfers between devices, on_device(): received = lax.all_to_all(sent, 'mer', 0, 0)  8.31 us
    ppermute x2, waiting for transfers between devices, from_behind(): lax.ppermute(block, axis, [((i - distance) % size, i) for i in range(size)])  6.19 us
    ppermute x2, starting transfers between devices, from_behind(): lax.ppermute(block, axis, [((i - distance) % size, i) for i in range(size)])  5.73 us
    pallas_call x1, Pallas kernels, on_device(): pl.pallas_call(element_kernel, out_shape=(shape(GROUPS, PAD, WINDOW), sha...  3.81 us
    pallas_call x1, Pallas kernels, on_device(): pl.pallas_call(gather_kernel, out_shape=(shape(3, 6 * PAD, OWN), shape(2...  2.27 us
    all_to_all x1, waiting for transfers between devices, on_device(): received = lax.all_to_all(sent, 'mer', 0, 0)  2.25 us
    pallas_call x1, Pallas kernels, on_device(): pl.pallas_call(span_kernel, out_shape=(shape(DOF, 2, OWN), shape(2, MOST)...  1.9 us
    unnamed x8, local copies, waits for them, and re-layouts  1.27 us
  transfers between devices with their start and end apart: 3, of which 3 were waited for; matrix products, arithmetic and copies ran while one was open for 0% of the time, Pallas kernels for 0%

profile of v1, /device:TPU:1, one launch (start us, length us, event | category | flops | bytes accessed | tf_op | source)
XLA Modules:
  0.0 33.0 jit_solution(7512637089351013351)
XLA Ops:
  0.6 2.3 %shard_map.122 = (f32[3,48,256]{2,1,0:T(8,128)}, f32[16,256]{1,0:T(8,128)}, f32[80,256]{1,0:T(8,128)}) custom-call(f32[3,6,2,4096]{3,2,1,0:T(2,128)} %modes.1, f32[6,2,256]{2,1,0:T(2,128)} %adjoint.1), custom_call_target="tpu_custom_call" | custom-call | tf_op jit(solution)/shard_map/pallas_call | solution.py:313
  2.9 5.7 %collective-permute-start = (f32[80,256]{1,0:T(8,128)}, f32[80,256]{1,0:T(8,128)S(1)}, u32[]{:S(2)}, u32[]{:S(2)}) collective-permute-start(f32[80,256]{1,0:T(8,128)} %get-tuple-element.10), channel_id=1, source_target_pairs={{16,0},{32,16},{48,32},{64,48},{80,64},{96,80},{112,96},{0,112},{1... | collective-permute-start | bytes 245768 | tf_op jit(solution)/shard_map/ppermute | solution.py:297
  9.2 1.2 %collective-permute-done.rim = f32[80,256]{1,0:T(8,128)S(1)} collective-permute-done((f32[80,256]{1,0:T(8,128)}, f32[80,256]{1,0:T(8,128)S(1)}, u32[]{:S(2)}, u32[]{:S(2)}) %collective-permute-start) | collective-permute-done | bytes 81952 | tf_op jit(solution)/shard_map/ppermute | solution.py:297
  10.4 0.0 copy-start.1
  10.4 0.6 %copy-done.1 = f32[80,256]{1,0:T(8,128)} copy-done((f32[80,256]{1,0:T(8,128)}, f32[80,256]{1,0:T(8,128)S(1)}, u32[]{:S(2)}) %copy-start.1) | copy-done | bytes 81944
  11.0 3.8 %shard_map.123 = (f32[16,8,128]{2,1,0:T(8,128)}, f32[16,256]{1,0:T(8,128)}, f32[8,256]{1,0:T(8,128)}) custom-call(f32[3,48,256]{2,1,0:T(8,128)} %get-tuple-element.8.own, f32[16,256]{1,0:T(8,128)} %get-tuple-element.9.own_adjoint, f32[80,256]{1,0:T(8,128)} %copy-done.1, s32[32,128]{1,0:T(8,128)} %bitcast.3, f32[2,4096]{1,0:T(2,128)} %thickness.1, ...), custom_call_target="tpu_custom_call" | custom-call | tf_op jit(solution)/shard_map/pallas_call | solution.py:321
  14.8 0.0 copy-start.3
  14.8 8.3 %all-to-all-start = ((f32[16,8,128]{2,1,0:T(8,128)}), f32[16,8,128]{2,1,0:T(8,128)S(1)}, u32[]{:S(2)}, u32[]{:S(2)}) async-start(f32[16,8,128]{2,1,0:T(8,128)} %get-tuple-element.11), calls=%async_computation | async-start | bytes 131072 | tf_op jit(solution)/shard_map/all_to_all | solution.py:346
  23.1 0.0 copy-done.3
  23.1 0.1 collective-permute-start.1
  23.2 5.0 %collective-permute-done.1.carry = f32[8,256]{1,0:T(8,128)S(1)} collective-permute-done((f32[8,256]{1,0:T(8,128)S(1)}, f32[8,256]{1,0:T(8,128)S(1)}, u32[]{:S(2)}, u32[]{:S(2)}) %collective-permute-start.1) | collective-permute-done | bytes 8224 | tf_op jit(solution)/shard_map/ppermute | solution.py:297
  28.2 0.0 copy-start.2
  28.3 2.2 %all-to-all-done.received = f32[16,8,128]{2,1,0:T(8,128)S(1)} async-done(((f32[16,8,128]{2,1,0:T(8,128)}), f32[16,8,128]{2,1,0:T(8,128)S(1)}, u32[]{:S(2)}, u32[]{:S(2)}) %all-to-all-start) | async-done | bytes 65568 | tf_op jit(solution)/shard_map/all_to_all | solution.py:346
  30.5 0.0 copy-start
  30.5 0.0 copy-done.2
  30.5 0.6 %copy-done = f32[16,8,128]{2,1,0:T(8,128)} copy-done((f32[16,8,128]{2,1,0:T(8,128)}, f32[16,8,128]{2,1,0:T(8,128)S(1)}, u32[]{:S(2)}) %copy-start) | copy-done | bytes 65560
  31.1 1.9 %shard_map.124 = (f32[6,2,256]{2,1,0:T(2,128)}, f32[2,768]{1,0:T(2,128)}) custom-call(f32[16,8,128]{2,1,0:T(8,128)} %copy-done, f32[16,256]{1,0:T(8,128)} %get-tuple-element.12.loads, f32[8,256]{1,0:T(8,128)} %copy-done.2, s32[1,16]{1,0:T(1,128)} %spans.3), custom_call_target="tpu_custom_call" | custom-call | tf_op jit(solution)/shard_map/pallas_call | solution.py:347
Async XLA Ops:
  2.9 7.5 %collective-permute-start = (f32[80,256]{1,0:T(8,128)}, f32[80,256]{1,0:T(8,128)S(1)}, u32[]{:S(2)}, u32[]{:S(2)}) collective-permute-start(f32[80,256]{1,0:T(8,128)} %get-tuple-element.10), channel_id=1, source_target_pairs={{16,0},{32,16},{48,32},{64,48},{80,64},{96,80},{112,96},{0,112},{1... | collective-permute-start | bytes 245768 | tf_op jit(solution)/shard_map/ppermute | solution.py:297
  10.4 0.6 %copy-start.1 = (f32[80,256]{1,0:T(8,128)}, f32[80,256]{1,0:T(8,128)S(1)}, u32[]{:S(2)}) copy-start(f32[80,256]{1,0:T(8,128)S(1)} %collective-permute-done.rim) | copy-start | bytes 245764
  14.8 8.3 %copy-start.3 = (f32[8,256]{1,0:T(8,128)S(1)}, f32[8,256]{1,0:T(8,128)}, u32[]{:S(2)}) copy-start(f32[8,256]{1,0:T(8,128)} %get-tuple-element.13) | copy-start | bytes 24580
  14.8 15.7 %all-to-all-start = ((f32[16,8,128]{2,1,0:T(8,128)}), f32[16,8,128]{2,1,0:T(8,128)S(1)}, u32[]{:S(2)}, u32[]{:S(2)}) async-start(f32[16,8,128]{2,1,0:T(8,128)} %get-tuple-element.11), calls=%async_computation | async-start | bytes 131072 | tf_op jit(solution)/shard_map/all_to_all | solution.py:346
  23.1 5.1 %collective-permute-start.1 = (f32[8,256]{1,0:T(8,128)S(1)}, f32[8,256]{1,0:T(8,128)S(1)}, u32[]{:S(2)}, u32[]{:S(2)}) collective-permute-start(f32[8,256]{1,0:T(8,128)S(1)} %copy-done.3), channel_id=1, source_target_pairs={{112,0},{0,16},{16,32},{32,48},{48,64},{64,80},{80,96},{96,112},{1... | collective-permute-start | bytes 24584 | tf_op jit(solution)/shard_map/ppermute | solution.py:297
  28.2 2.3 %copy-start.2 = (f32[8,256]{1,0:T(8,128)}, f32[8,256]{1,0:T(8,128)S(1)}, u32[]{:S(2)}) copy-start(f32[8,256]{1,0:T(8,128)S(1)} %collective-permute-done.1.carry) | copy-start | bytes 24580
  30.5 0.6 %copy-start = (f32[16,8,128]{2,1,0:T(8,128)}, f32[16,8,128]{2,1,0:T(8,128)S(1)}, u32[]{:S(2)}) copy-start(f32[16,8,128]{2,1,0:T(8,128)S(1)} %all-to-all-done.received) | copy-start | bytes 196612

commit v2 on v1

v2 whole, which is shorter than its diff:
```python
import jax
import jax.numpy as jnp
from jax import lax
from jax.experimental import pallas as pl
from jax.experimental.pallas import tpu as pltpu
from jax.sharding import PartitionSpec as P


DOF = 6
SMALL = 8
PAD = 8
OWN = 256
GROUPS = 16
COLUMN = OWN * GROUPS
MOST = 768
LANES = 128
ROWS = COLUMN // LANES
WINDOW = 128
HALF = 64

f32, bf16, i32 = jnp.float32, jnp.bfloat16, jnp.int32
vmem = pl.BlockSpec(memory_space=pltpu.VMEM)
smem = pl.BlockSpec(memory_space=pltpu.SMEM)
hbm = pl.BlockSpec(memory_space=pltpu.HBM)
small = pltpu.CompilerParams(vmem_limit_bytes=12 << 20)


def iota(shape, axis):
    return lax.broadcasted_iota(i32, shape, axis)


def parts(x):
    high = x.astype(bf16)
    rest = x - high.astype(f32)
    middle = rest.astype(bf16)
    low = (rest - middle.astype(f32)).astype(bf16)
    return high, middle, low


def matmul(a, b):
    return jnp.dot(a, b, preferred_element_type=f32)


def matmul_nt(a, b):
    return lax.dot_general(a, b, (((1,), (1,)), ((), ())), preferred_element_type=f32)


def left_stack(three, axis):
    high, middle, low = three
    return jnp.concatenate([high, high, middle, middle, high, low], axis=axis)


def right_stack(three, axis):
    high, middle, low = three
    return jnp.concatenate([high, middle, high, middle, low, high], axis=axis)


def gather_kernel(modes, adjoint, *rest):
    small_in, rest = rest[:SMALL], rest[SMALL:]
    own, own_adjoint, rim, *rest = rest
    small_out, (held, held_adjoint, sems) = rest[:SMALL], rest[SMALL:]
    member = lax.axis_index("mer")
    copies = []
    for d in range(3):
        block = (member + (d + GROUPS - 1)) & (GROUPS - 1)
        columns = pl.ds(pl.multiple_of(block * OWN, OWN), OWN)
        copies.append(pltpu.make_async_copy(modes.at[:, :, :, columns], held.at[d], sems.at[d]))
    copies.append(pltpu.make_async_copy(adjoint, held_adjoint, sems.at[3]))
    for i in range(SMALL):
        copies.append(pltpu.make_async_copy(small_in[i], small_out[i], sems.at[4 + i]))
    for copy in copies:
        copy.start()
    own[...] = jnp.zeros_like(own)
    own_adjoint[...] = jnp.zeros_like(own_adjoint)
    rim[...] = jnp.zeros_like(rim)
    for d in range(3):
        copies[d].wait()
        for f in range(3):
            for i in range(DOF):
                pair = held[d, f, i]
                rim[(3 * d + f) * PAD + i : (3 * d + f) * PAD + i + 1, :] = pair[0:1]
                own[d, f * PAD + i : f * PAD + i + 1, :] = pair[0:1]
                own[d, (3 + f) * PAD + i : (3 + f) * PAD + i + 1, :] = pair[1:2]
    for copy in copies[3:]:
        copy.wait()
    for i in range(DOF):
        pair = held_adjoint[i]
        rim[9 * PAD + i : 9 * PAD + i + 1, :] = pair[0:1]
        own_adjoint[i : i + 1, :] = pair[0:1]
        own_adjoint[PAD + i : PAD + i + 1, :] = pair[1:2]


def fold(x):
    return (x[0:8] + x[8:16]) + (x[16:24] + x[24:32])


def column_sum(x):
    return jnp.sum(x, axis=0, keepdims=True)


def cycle_terms(corner_parts, adjoint, growth, thick, weights):
    bend = [3.0 * t * t for t in thick]
    pair_weights = weights[64:160]
    prestate_weights = jnp.concatenate([weights[0:64], weights[160:176]], axis=0)
    outcome = {}
    for d in (1, 0):
        stiff = jnp.zeros((PAD, OWN), f32)
        pairs = [jnp.zeros((PAD, OWN), f32)] * 3
        for f in range(2):
            three = corner_parts(f, d)
            value = (three[0] + three[1]) + three[2]
            stack = right_stack([t.astype(bf16) for t in three], 0)
            if d == 1:
                product = matmul(weights[0:160], stack)
                stiff = stiff + fold(value * (product[0:32] + bend[d] * product[32:64]))
                product = product[64:160]
            else:
                product = matmul(pair_weights, stack)
            pairs = [pairs[s] + fold(value * product[32 * s : 32 * s + 32]) for s in range(3)]
        pairs = [column_sum(x) for x in pairs]
        stack = right_stack([t.astype(bf16) for t in corner_parts(2, d)], 0)
        product = matmul(prestate_weights, stack)
        tangent = product[0:32] + bend[d] * product[32:64]
        if d == 1:
            aterm = column_sum(adjoint[0] * tangent[0:8] + adjoint[1] * tangent[8:16])
            coupling = (
                product[64:65] * pairs[0] + product[65:66] * pairs[1]
            ) + product[66:67] * pairs[2]
            rows = [growth[d] * (column_sum(stiff) - aterm), growth[d] * coupling]
        else:
            aterm = column_sum(adjoint[0] * tangent[24:32] + adjoint[1] * tangent[16:24])
            rows.append(-(growth[d] * aterm))
        outcome[d] = [thick[d] * x for x in pairs] + [jnp.zeros((5, OWN), f32)]
    return rows, jnp.concatenate(outcome[0] + outcome[1], axis=0)


def corner_rows():
    entry = iota((32, 24), 1)
    return (iota((32, 24), 0) == (entry // 6) * PAD + entry % 6).astype(f32).astype(bf16)


def stored_order(rows, order):
    n = rows.shape[0]
    placed = matmul_nt(jnp.concatenate(parts(rows), axis=0), order)
    return (placed[0:n] + placed[n : 2 * n]) + placed[2 * n : 3 * n]


def local_kernel(
    own,
    own_adjoint,
    slots,
    thickness,
    weld,
    membrane,
    bending,
    geometric,
    stress_map,
    order,
    second,
    second_adjoint,
    weights,
    scalings,
    gradients,
    pairs,
    thick_rows,
    weld_rows,
    nodes,
):
    member = lax.axis_index("mer")

    lane = iota((1, OWN), 1)
    position = [(lane * GROUPS + (member + d - 1)) & (COLUMN - 1) for d in range(3)]
    pick = [
        (iota((LANES, OWN), 0) == (position[d] & (LANES - 1))).astype(f32).astype(bf16)
        for d in range(3)
    ]
    for a in range(ROWS):
        thick_rows[2 * a : 2 * a + 2, :] = thickness[:, a * LANES : (a + 1) * LANES]
        weld_rows[2 * a : 2 * a + 2, :] = weld[:, a * LANES : (a + 1) * LANES]
    thick_parts = parts(thick_rows[...])
    weld_part = weld_rows[...].astype(f32).astype(bf16)
    slot_part = (slots[...] & (OWN - 1)).astype(f32).astype(bf16)

    def choose(rows, d, stride, offset):
        here = iota(rows.shape, 0) == (position[d] >> 7) * stride + offset
        return column_sum(jnp.where(here, rows, 0.0))

    growth, thick = {}, {}
    stacked = jnp.concatenate([*thick_parts, weld_part], axis=0)
    for d in range(2):
        rows = matmul(stacked, pick[d])
        thick_all = (rows[0:64] + rows[64:128]) + rows[128:192]
        for r in range(2):
            growth[d, r] = 1.0 + 0.5 * choose(rows[192:256], d, 2, r)
            thick[d, r] = choose(thick_all, d, 2, r) * growth[d, r]
    scalings[...] = jnp.concatenate(
        [growth[0, 1], growth[1, 1], thick[0, 1], thick[1, 1], jnp.zeros((4, OWN), f32)], axis=0
    )

    for d in range(3):
        slot = choose(matmul(slot_part, pick[d]), d, 1, 0).astype(i32)
        order[d] = (iota((OWN, OWN), 0) == slot).astype(f32).astype(bf16)
        values = own[d]
        if d == 1:
            values = jnp.concatenate([values, own_adjoint[...]], axis=0)
        count = values.shape[0]
        placed = matmul(jnp.concatenate(parts(values), axis=0), order[d])
        for p in range(3):
            nodes[d, p, 0:count, :] = placed[p * count : (p + 1) * count]
            second[d, p] = placed[p * count + 24 : p * count + 48]

    spread = (
        iota((24, 32), 1) == (iota((24, 32), 0) // 6) * PAD + iota((24, 32), 0) % 6
    ).astype(f32).astype(bf16)
    spread_t = corner_rows()
    stress_rows = jnp.concatenate([stress_map[...], jnp.zeros((5, 24), f32)], axis=0)
    matrices = [membrane[...], bending[...], geometric[0], geometric[1], geometric[2]]
    pieces = [[], [], []]
    for matrix in matrices:
        for p, part in enumerate(parts(matrix)):
            wide = matmul(part, spread).astype(bf16)
            pieces[p].append(matmul(spread_t, wide))
    for p, part in enumerate(parts(stress_rows)):
        pieces[p].append(matmul(part, spread))
        pieces[p].append(jnp.zeros((PAD, 32), f32))
    weights[...] = left_stack([jnp.concatenate(w, axis=0).astype(bf16) for w in pieces], 1)

    def corner_parts(f, d):
        low, high = f * PAD, (f + 3) * PAD
        return [
            jnp.concatenate(
                [
                    nodes[d, p, low : low + PAD, :],
                    nodes[d, p, high : high + PAD, :],
                    nodes[d + 1, p, high : high + PAD, :],
                    nodes[d + 1, p, low : low + PAD, :],
                ],
                axis=0,
            )
            for p in range(3)
        ]

    adjoint = [
        (nodes[1, 0, g : g + PAD, :] + nodes[1, 1, g : g + PAD, :]) + nodes[1, 2, g : g + PAD, :]
        for g in (48, 56)
    ]
    second_adjoint[...] = adjoint[1]
    rows, pair_rows = cycle_terms(
        corner_parts,
        adjoint,
        [growth[d, 0] for d in range(2)],
        [thick[d, 0] for d in range(2)],
        weights[...],
    )
    gradients[...] = jnp.concatenate(rows + [jnp.zeros((5, OWN), f32)], axis=0)
    pairs[...] = pair_rows


def rim_kernel(
    rim,
    order,
    second,
    second_adjoint,
    weights,
    scalings,
    gradients,
    spans,
    sent,
    pairs,
    nodes,
    counts,
    sem,
):
    fetch = pltpu.make_async_copy(spans, counts, sem)
    fetch.start()
    for d in range(3):
        values = rim[3 * d * PAD : 3 * (d + 1) * PAD, :]
        if d == 1:
            values = jnp.concatenate([values, rim[9 * PAD : 10 * PAD, :]], axis=0)
        count = values.shape[0]
        placed = matmul(jnp.concatenate(parts(values), axis=0), order[d])
        for p in range(3):
            nodes[d, p, 0:count, :] = placed[p * count : (p + 1) * count]

    def corner_parts(f, d):
        rows = slice(f * PAD, (f + 1) * PAD)
        return [
            jnp.concatenate(
                [
                    second[d, p, rows, :],
                    nodes[d, p, rows, :],
                    nodes[d + 1, p, rows, :],
                    second[d + 1, p, rows, :],
                ],
                axis=0,
            )
            for p in range(3)
        ]

    adjoint = [second_adjoint[...], (nodes[1, 0, 24:32, :] + nodes[1, 1, 24:32, :]) + nodes[1, 2, 24:32, :]]
    rows, pair_rows = cycle_terms(
        corner_parts,
        adjoint,
        [scalings[0:1, :], scalings[1:2, :]],
        [scalings[2:3, :], scalings[3:4, :]],
        weights[...],
    )
    pairs[...] = pair_rows

    odd = (lax.axis_index("mer") & 1) == 1
    none = jnp.zeros((1, OWN), f32)

    def four_of_eight(four):
        return jnp.concatenate(
            [jnp.where(odd, 0.0, x) for x in four] + [jnp.where(odd, x, 0.0) for x in four], axis=0
        )

    now = four_of_eight([gradients[0:1, :], rows[0], gradients[1:2, :], rows[1]])
    late = four_of_eight([gradients[2:3, :], rows[2], none, none])
    lower = iota((PAD, WINDOW), 1) < HALF
    fetch.wait()
    start = jnp.int32(0)
    for target in range(GROUPS):
        first = (start >> 4) & (OWN - 1)
        turned = pltpu.roll(now, (OWN - first) & (OWN - 1), 1)
        turned_late = pltpu.roll(late, (OWN + HALF - first) & (OWN - 1), 1)
        sent[target] = jnp.where(lower, turned[:, 0:WINDOW], turned_late[:, 0:WINDOW])
        start = start + counts[0, target]


def load_kernel(first_pairs, second_pairs, order, stress_map, factor, loads, carry):
    stress_rows = jnp.concatenate([stress_map[...], jnp.zeros((5, 24), f32)], axis=0)
    spread_t = corner_rows()
    load_weights = left_stack([matmul_nt(spread_t, part).astype(bf16) for part in parts(stress_rows)], 1)
    lower, upper = [], []
    for pairs in (first_pairs, second_pairs):
        before = matmul(load_weights, right_stack(parts(pairs[0:PAD, :]), 0))
        here = matmul(load_weights, right_stack(parts(pairs[PAD : 2 * PAD, :]), 0))
        lower.append(here[0:8] + before[24:32])
        upper.append(here[8:16] + before[16:24])
    stored = stored_order(jnp.concatenate([lower[0], upper[0] + lower[1], upper[1]], axis=0), order[1])
    stored = factor[0] * stored
    loads[...] = stored[0 : 2 * PAD]
    carry[...] = stored[2 * PAD : 3 * PAD]


def place_kernel(spans, spread_now, spread_late, sources):
    member = lax.axis_index("mer")
    group = iota((1, GROUPS), 1)
    start = jnp.sum(jnp.where(group < member, spans[...], 0), axis=1, keepdims=True)
    count = jnp.sum(jnp.where(group == member, spans[...], 0), axis=1, keepdims=True)
    element = iota((1, MOST), 1) + (start & (GROUPS - 1))
    valid = iota((1, MOST), 1) < count
    for late, spread_ref in ((0, spread_now), (1, spread_late)):
        sources[late : late + 1, :] = jnp.where(valid, (element + late) & (GROUPS - 1), -1)
        third = (iota((HALF, MOST), 0) == ((element + late) >> 4)).astype(f32).astype(bf16)
        for p in range(3):
            spread_ref[p * HALF : (p + 1) * HALF, :] = third


def span_kernel(received, loads, carry, spread_now, spread_late, sources, factor, adjoint_load, thickness_grad):
    values = jnp.concatenate([received[2 * g] + received[2 * g + 1] for g in range(GROUPS // 2)], axis=0)
    lower_half = iota((PAD, MOST), 0) < 4
    both = []
    for late, spread_ref in ((0, spread_now), (1, spread_late)):
        stack = jnp.concatenate(parts(values[:, late * HALF : (late + 1) * HALF]), axis=1)
        rows = matmul(stack, spread_ref[...])
        source = sources[late : late + 1, :]
        wanted = jnp.where(lower_half, source, source - 1)
        picked = jnp.zeros((PAD, MOST), f32)
        for g in range(GROUPS // 2):
            picked = jnp.where(wanted == 2 * g, rows[g * PAD : (g + 1) * PAD], picked)
        both.append(picked[0:4] + picked[4:8])
    thickness_grad[...] = (both[0][0:2] - factor[0] * both[0][2:4]) + both[1][0:2]

    first = loads[0:PAD, :] + carry[...]
    second = loads[PAD : 2 * PAD, :]
    for i in range(DOF):
        adjoint_load[i, 0:1, :] = first[i : i + 1]
        adjoint_load[i, 1:2, :] = second[i : i + 1]


def shape(*dims, dtype=f32):
    return jax.ShapeDtypeStruct(dims, dtype)


def from_behind(block, axis, distance):
    size = lax.axis_size(axis)
    return lax.ppermute(block, axis, [((i - distance) % size, i) for i in range(size)])


def on_device(
    adjoint,
    mode_fields,
    node_slot,
    thickness,
    weld_land,
    panel_spans,
    load_factor,
    membrane,
    bending,
    geometric,
    stress_map,
):
    brought = (node_slot.reshape(ROWS, LANES), thickness, weld_land, membrane, bending, geometric, stress_map, panel_spans)
    own, own_adjoint, rim, *brought = pl.pallas_call(
        gather_kernel,
        out_shape=(shape(3, 6 * PAD, OWN), shape(2 * PAD, OWN), shape(10 * PAD, OWN))
        + tuple(shape(*x.shape, dtype=x.dtype) for x in brought),
        in_specs=[hbm] * (2 + SMALL),
        out_specs=(vmem,) * (3 + SMALL),
        scratch_shapes=[
            pltpu.VMEM((3, 3, DOF, 2, OWN), f32),
            pltpu.VMEM((DOF, 2, OWN), f32),
            pltpu.SemaphoreType.DMA((4 + SMALL,)),
        ],
        compiler_params=small,
    )(*[pltpu.with_memory_space_constraint(x, pltpu.HBM) for x in (mode_fields, adjoint, *brought)])
    *brought, panel_spans = brought
    stress_map = brought[-1]
    rim = from_behind(rim, "circ", -1)
    order, *kept, first_pairs = pl.pallas_call(
        local_kernel,
        out_shape=(
            shape(3, OWN, OWN, dtype=bf16),
            shape(3, 3, 3 * PAD, OWN),
            shape(PAD, OWN),
            shape(176, 192, dtype=bf16),
            shape(PAD, OWN),
            shape(PAD, OWN),
            shape(2 * PAD, OWN),
        ),
        in_specs=[vmem] * 9,
        out_specs=(vmem,) * 7,
        scratch_shapes=[
            pltpu.VMEM((2 * ROWS, LANES), f32),
            pltpu.VMEM((2 * ROWS, LANES), i32),
            pltpu.VMEM((3, 3, 8 * PAD, OWN), f32),
        ],
        compiler_params=small,
    )(own, own_adjoint, *brought)
    sent, second_pairs = pl.pallas_call(
        rim_kernel,
        out_shape=(shape(GROUPS, PAD, WINDOW), shape(2 * PAD, OWN)),
        in_specs=[vmem] * 8,
        out_specs=(vmem,) * 2,
        scratch_shapes=[
            pltpu.VMEM((3, 3, 4 * PAD, OWN), f32),
            pltpu.SMEM((1, GROUPS), i32),
            pltpu.SemaphoreType.DMA,
        ],
        compiler_params=small,
    )(rim, order, *kept, panel_spans)
    received = lax.all_to_all(sent, "mer", 0, 0)
    second_pairs, factor = lax.optimization_barrier((second_pairs, load_factor.reshape(1)))
    loads, carry = pl.pallas_call(
        load_kernel,
        out_shape=(shape(2 * PAD, OWN), shape(PAD, OWN)),
        in_specs=[vmem] * 4 + [smem],
        out_specs=(vmem,) * 2,
        compiler_params=small,
    )(first_pairs, second_pairs, order, stress_map, factor)
    carry = from_behind(carry, "circ", 1)
    places = pl.pallas_call(
        place_kernel,
        out_shape=(shape(3 * HALF, MOST, dtype=bf16), shape(3 * HALF, MOST, dtype=bf16), shape(2, MOST, dtype=i32)),
        in_specs=[vmem],
        out_specs=(vmem,) * 3,
        compiler_params=small,
    )(panel_spans)
    return pl.pallas_call(
        span_kernel,
        out_shape=(shape(DOF, 2, OWN), shape(2, MOST)),
        in_specs=[vmem] * 6 + [smem],
        out_specs=(vmem,) * 2,
        compiler_params=small,
    )(received, loads, carry, *places, factor)


def solution(mesh):
    return jax.shard_map(
        on_device,
        mesh=mesh,
        in_specs=(
            P(None, "circ", "mer"),
            P(None, None, "circ", None),
            P(),
            P("circ", None),
            P("circ", None),
            P("circ", None),
            P(),
            P(),
            P(),
            P(),
            P(),
        ),
        out_specs=(P(None, "circ", "mer"), P("circ", "mer")),
        check_vma=False,
    )
```

time: 33.4 us -> 26.9 us (0.81)
  Pallas kernels: 7.97 us -> 5.13 us
  waiting for transfers between devices: 8.43 us -> 6.28 us
  local copies, waits for them, and re-layouts: 1.27 us -> 0 us
    unnamed x8 -> x0, local copies, waits for them, and re-layouts: 1.27 us -> none
    pallas_call x1, Pallas kernels: 2.27 us -> 1.05 us  [on_device(): pl.pallas_call(gather_kernel, out_shape=(shape(3, 6 * PAD, OWN), shape(2...]
    ppermute x2, waiting for transfers between devices: 6.19 us -> 5.06 us  [from_behind(): lax.ppermute(block, axis, [((i - distance) % size, i) for i in range(size)])]
    pallas_call x1, Pallas kernels: 1.9 us -> 0.87 us  [on_device(): pl.pallas_call(span_kernel, out_shape=(shape(DOF, 2, OWN), shape(2, MOST)...]
    all_to_all x1, waiting for transfers between devices: 2.25 us -> 1.22 us  [on_device(): received = lax.all_to_all(sent, 'mer', 0, 0)]
    pallas_call x1 -> x4, Pallas kernels: 3.81 us -> 3.2 us  [the longest x1 1.38 us: on_device(): pl.pallas_call(rim_kernel, out_shape=(shape(GROUPS, PAD, WINDOW), shape(2...]
  transfers between devices with their start and end apart: 3 -> 3, of which waited for: 3 -> 3; matrix products, arithmetic and copies ran while one was open for 0% -> 0% of each run, Pallas kernels for 0% -> 7%
where the time goes in v2:
time: 26.9 us; the launch traced here: 26.7 us
  starting transfers between devices  13.9 us (52%)
  waiting for transfers between devices  6.28 us (23%)
  Pallas kernels  5.13 us (19%)
  between operations  1.33 us (5%)
    all_to_all x1, starting transfers between devices, on_device(): received = lax.all_to_all(sent, 'mer', 0, 0)  8.19 us
    ppermute x2, starting transfers between devices, from_behind(): lax.ppermute(block, axis, [((i - distance) % size, i) for i in range(size)])  5.73 us
    ppermute x2, waiting for transfers between devices, from_behind(): lax.ppermute(block, axis, [((i - distance) % size, i) for i in range(size)])  5.06 us
    pallas_call x1, Pallas kernels, on_device(): pl.pallas_call(rim_kernel, out_shape=(shape(GROUPS, PAD, WINDOW), shape(2...  1.38 us
    all_to_all x1, waiting for transfers between devices, on_device(): received = lax.all_to_all(sent, 'mer', 0, 0)  1.22 us
    pallas_call x1, Pallas kernels, on_device(): pl.pallas_call(local_kernel, out_shape=(shape(3, OWN, OWN, dtype=bf16), s...  1.16 us
    pallas_call x1, Pallas kernels, on_device(): pl.pallas_call(gather_kernel, out_shape=(shape(3, 6 * PAD, OWN), shape(2...  1.05 us
    pallas_call x1, Pallas kernels, on_device(): pl.pallas_call(span_kernel, out_shape=(shape(DOF, 2, OWN), shape(2, MOST)...  0.87 us
  transfers between devices with their start and end apart: 3, of which 3 were waited for; matrix products, arithmetic and copies ran while one was open for 0% of the time, Pallas kernels for 7%

profile of v2, /device:TPU:1, one launch (start us, length us, event | category | flops | bytes accessed | tf_op | source)
XLA Modules:
  0.0 26.7 jit_solution(17215096201227519517)
XLA Ops:
  0.6 1.1 %shard_map.122 = (f32[3,48,256]{2,1,0:T(8,128)S(1)}, f32[16,256]{1,0:T(8,128)S(1)}, f32[80,256]{1,0:T(8,128)S(1)}, s32[32,128]{1,0:T(8,128)S(1)}, f32[2,4096]{1,...) custom-call(f32[3,6,2,4096]{3,2,1,0:T(2,128)} %modes.1, ...), custom_call_target="tpu_custom_call" | custom-call | tf_op jit(solution)/shard_map/pallas_call | solution.py:406
  1.7 5.7 %collective-permute-start = (f32[80,256]{1,0:T(8,128)S(1)}, f32[80,256]{1,0:T(8,128)S(1)}, u32[]{:S(2)}, u32[]{:S(2)}) collective-permute-start(f32[80,256]{1,0:T(8,128)S(1)} %get-tuple-element.29), channel_id=1, source_target_pairs={{16,0},{32,16},{48,32},{64,48},{80,64},{96,80},{112,96},{0,112},{1... | collective-permute-start | bytes 245768 | tf_op jit(solution)/shard_map/ppermute | solution.py:389
  7.3 1.2 %shard_map.123 = (bf16[3,256,256]{2,1,0:T(8,128)(2,1)S(1)}, f32[3,3,24,256]{3,2,1,0:T(8,128)S(1)}, f32[8,256]{1,0:T(8,128)S(1)}, bf16[176,192]{1,0:T(8,128)(2,1)...) custom-call(f32[3,48,256]{2,1,0:T(8,128)S(1)} %get-tuple-element.30.own, ...), custom_call_target="tpu_custom_call" | custom-call | tf_op jit(solution)/shard_map/pallas_call | solution.py:422
  8.5 0.3 %collective-permute-done.rim = f32[80,256]{1,0:T(8,128)S(1)} collective-permute-done((f32[80,256]{1,0:T(8,128)S(1)}, f32[80,256]{1,0:T(8,128)S(1)}, u32[]{:S(2)}, u32[]{:S(2)}) %collective-permute-start) | collective-permute-done | bytes 81952 | tf_op jit(solution)/shard_map/ppermute | solution.py:389
  8.8 1.4 %shard_map.124 = (f32[16,8,128]{2,1,0:T(8,128)}, f32[16,256]{1,0:T(8,128)S(1)}) custom-call(f32[80,256]{1,0:T(8,128)S(1)} %collective-permute-done.rim, bf16[3,256,256]{2,1,0:T(8,128)(2,1)S(1)} %get-tuple-element.39.order, f32[3,3,24,256]{3,2,1,0:T(8,128)S(1)} %get-tuple-element.40.second, f32[8,256]{1,0:T(8,128)S(1)} %get-tuple-element.41.second_adjoint, ...), custom_call_target="tpu_custom_call" | custom-call | tf_op jit(solution)/shard_map/pallas_call | solution.py:442
  10.2 8.2 %all-to-all-start = ((f32[16,8,128]{2,1,0:T(8,128)}), f32[16,8,128]{2,1,0:T(8,128)S(1)}, u32[]{:S(2)}, u32[]{:S(2)}) async-start(f32[16,8,128]{2,1,0:T(8,128)} %get-tuple-element.46), calls=%async_computation | async-start | bytes 131072 | tf_op jit(solution)/shard_map/all_to_all | solution.py:454
  19.1 0.5 %shard_map.125 = (f32[16,256]{1,0:T(8,128)S(1)}, f32[8,256]{1,0:T(8,128)S(1)}) custom-call(f32[16,256]{1,0:T(8,128)S(1)} %get-tuple-element.47.first_pairs, f32[16,256]{1,0:T(8,128)S(1)} %get-tuple-element.49.second_pairs, bf16[3,256,256]{2,1,0:T(8,128)(2,1)S(1)} %get-tuple-element.39.order, f32[3,24]{1,0:T(4,128)S(1)} %get-tuple-element.38.stress_map, ...), custom_call_target="tpu_custom_call" | custom-call | tf_op jit(solution)/shard_map/pallas_call | solution.py:456
  19.6 0.1 collective-permute-start.1
  19.6 0.2 shard_map.126
  19.8 4.7 %collective-permute-done.1.carry = f32[8,256]{1,0:T(8,128)S(1)} collective-permute-done((f32[8,256]{1,0:T(8,128)S(1)}, f32[8,256]{1,0:T(8,128)S(1)}, u32[]{:S(2)}, u32[]{:S(2)}) %collective-permute-start.1) | collective-permute-done | bytes 8224 | tf_op jit(solution)/shard_map/ppermute | solution.py:389
  24.6 1.2 %all-to-all-done.received = f32[16,8,128]{2,1,0:T(8,128)S(1)} async-done(((f32[16,8,128]{2,1,0:T(8,128)}), f32[16,8,128]{2,1,0:T(8,128)S(1)}, u32[]{:S(2)}, u32[]{:S(2)}) %all-to-all-start) | async-done | bytes 65568 | tf_op jit(solution)/shard_map/all_to_all | solution.py:454
  25.8 0.9 %shard_map.127 = (f32[6,2,256]{2,1,0:T(2,128)}, f32[2,768]{1,0:T(2,128)}) custom-call(f32[16,8,128]{2,1,0:T(8,128)S(1)} %all-to-all-done.received, f32[16,256]{1,0:T(8,128)S(1)} %get-tuple-element.51.loads, f32[8,256]{1,0:T(8,128)S(1)} %collective-permute-done.1.carry, bf16[192,768]{1,0:T(8,128)(2,1)S(1)} %get-tuple-element.53.spread_now, ...), custom_call_target="tpu_custom_call" | custom-call | tf_op jit(solution)/shard_map/pallas_call | solution.py:471
Async XLA Ops:
  1.7 7.1 %collective-permute-start = (f32[80,256]{1,0:T(8,128)S(1)}, f32[80,256]{1,0:T(8,128)S(1)}, u32[]{:S(2)}, u32[]{:S(2)}) collective-permute-start(f32[80,256]{1,0:T(8,128)S(1)} %get-tuple-element.29), channel_id=1, source_target_pairs={{16,0},{32,16},{48,32},{64,48},{80,64},{96,80},{112,96},{0,112},{1... | collective-permute-start | bytes 245768 | tf_op jit(solution)/shard_map/ppermute | solution.py:389
  10.2 15.6 %all-to-all-start = ((f32[16,8,128]{2,1,0:T(8,128)}), f32[16,8,128]{2,1,0:T(8,128)S(1)}, u32[]{:S(2)}, u32[]{:S(2)}) async-start(f32[16,8,128]{2,1,0:T(8,128)} %get-tuple-element.46), calls=%async_computation | async-start | bytes 131072 | tf_op jit(solution)/shard_map/all_to_all | solution.py:454
  19.6 5.0 %collective-permute-start.1 = (f32[8,256]{1,0:T(8,128)S(1)}, f32[8,256]{1,0:T(8,128)S(1)}, u32[]{:S(2)}, u32[]{:S(2)}) collective-permute-start(f32[8,256]{1,0:T(8,128)S(1)} %get-tuple-element.52), channel_id=1, source_target_pairs={{112,0},{0,16},{16,32},{32,48},{48,64},{64,80},{80,96},{96,112},{1... | collective-permute-start | bytes 24584 | tf_op jit(solution)/shard_map/ppermute | solution.py:389

commit v3 on v2

--- a/solution.py
+++ b/solution.py
@@ -7,7 +7,7 @@
 
 
 DOF = 6
-SMALL = 8
+SMALL = 2
 PAD = 8
 OWN = 256
 GROUPS = 16
@@ -57,8 +57,8 @@
 
 def gather_kernel(modes, adjoint, *rest):
     small_in, rest = rest[:SMALL], rest[SMALL:]
-    own, own_adjoint, rim, *rest = rest
-    small_out, (held, held_adjoint, sems) = rest[:SMALL], rest[SMALL:]
+    held, held_adjoint, rim, *rest = rest
+    small_out, (sems,) = rest[:SMALL], rest[SMALL:]
     member = lax.axis_index("mer")
     copies = []
     for d in range(3):
@@ -70,24 +70,17 @@
         copies.append(pltpu.make_async_copy(small_in[i], small_out[i], sems.at[4 + i]))
     for copy in copies:
         copy.start()
-    own[...] = jnp.zeros_like(own)
-    own_adjoint[...] = jnp.zeros_like(own_adjoint)
-    rim[...] = jnp.zeros_like(rim)
+    rim[56:64, :] = jnp.zeros((PAD, OWN), f32)
     for d in range(3):
         copies[d].wait()
         for f in range(3):
             for i in range(DOF):
-                pair = held[d, f, i]
-                rim[(3 * d + f) * PAD + i : (3 * d + f) * PAD + i + 1, :] = pair[0:1]
-                own[d, f * PAD + i : f * PAD + i + 1, :] = pair[0:1]
-                own[d, (3 + f) * PAD + i : (3 + f) * PAD + i + 1, :] = pair[1:2]
+                row = (3 * d + f) * DOF + i
+                rim[row : row + 1, :] = held[d, f, i, 0:1, :]
     for copy in copies[3:]:
         copy.wait()
     for i in range(DOF):
-        pair = held_adjoint[i]
-        rim[9 * PAD + i : 9 * PAD + i + 1, :] = pair[0:1]
-        own_adjoint[i : i + 1, :] = pair[0:1]
-        own_adjoint[PAD + i : PAD + i + 1, :] = pair[1:2]
+        rim[54 + i : 55 + i, :] = held_adjoint[i, 0:1, :]
 
 
 def fold(x):
@@ -146,8 +139,8 @@
 
 
 def local_kernel(
-    own,
-    own_adjoint,
+    held,
+    held_adjoint,
     slots,
     thickness,
     weld,
@@ -165,6 +158,7 @@
     thick_rows,
     weld_rows,
     nodes,
+    own,
 ):
     member = lax.axis_index("mer")
 
@@ -197,13 +191,20 @@
         [growth[0, 1], growth[1, 1], thick[0, 1], thick[1, 1], jnp.zeros((4, OWN), f32)], axis=0
     )
 
+    own[...] = jnp.zeros_like(own)
+    for r in range(2):
+        for i in range(DOF):
+            for d in range(3):
+                for f in range(3):
+                    row = (f + 3 * r) * PAD + i
+                    own[d, row : row + 1, :] = held[d, f, i, r : r + 1, :]
+            row = (6 + r) * PAD + i
+            own[1, row : row + 1, :] = held_adjoint[i, r : r + 1, :]
     for d in range(3):
         slot = choose(matmul(slot_part, pick[d]), d, 1, 0).astype(i32)
         order[d] = (iota((OWN, OWN), 0) == slot).astype(f32).astype(bf16)
-        values = own[d]
-        if d == 1:
-            values = jnp.concatenate([values, own_adjoint[...]], axis=0)
-        count = values.shape[0]
+        count = 8 * PAD if d == 1 else 6 * PAD
+        values = own[d, 0:count, :]
         placed = matmul(jnp.concatenate(parts(values), axis=0), order[d])
         for p in range(3):
             nodes[d, p, 0:count, :] = placed[p * count : (p + 1) * count]
@@ -274,9 +275,8 @@
     fetch = pltpu.make_async_copy(spans, counts, sem)
     fetch.start()
     for d in range(3):
-        values = rim[3 * d * PAD : 3 * (d + 1) * PAD, :]
-        if d == 1:
-            values = jnp.concatenate([values, rim[9 * PAD : 10 * PAD, :]], axis=0)
+        groups = [3 * d, 3 * d + 1, 3 * d + 2] + [9] * (d == 1)
+        values = jnp.concatenate([rim[g * DOF : g * DOF + PAD, :] for g in groups], axis=0)
         count = values.shape[0]
         placed = matmul(jnp.concatenate(parts(values), axis=0), order[d])
         for p in range(3):
@@ -402,22 +402,17 @@
     geometric,
     stress_map,
 ):
-    brought = (node_slot.reshape(ROWS, LANES), thickness, weld_land, membrane, bending, geometric, stress_map, panel_spans)
-    own, own_adjoint, rim, *brought = pl.pallas_call(
+    brought = (stress_map, panel_spans)
+    held, held_adjoint, rim, *brought = pl.pallas_call(
         gather_kernel,
-        out_shape=(shape(3, 6 * PAD, OWN), shape(2 * PAD, OWN), shape(10 * PAD, OWN))
+        out_shape=(shape(3, 3, DOF, 2, OWN), shape(DOF, 2, OWN), shape(8 * PAD, OWN))
         + tuple(shape(*x.shape, dtype=x.dtype) for x in brought),
         in_specs=[hbm] * (2 + SMALL),
         out_specs=(vmem,) * (3 + SMALL),
-        scratch_shapes=[
-            pltpu.VMEM((3, 3, DOF, 2, OWN), f32),
-            pltpu.VMEM((DOF, 2, OWN), f32),
-            pltpu.SemaphoreType.DMA((4 + SMALL,)),
-        ],
+        scratch_shapes=[pltpu.SemaphoreType.DMA((4 + SMALL,))],
         compiler_params=small,
     )(*[pltpu.with_memory_space_constraint(x, pltpu.HBM) for x in (mode_fields, adjoint, *brought)])
-    *brought, panel_spans = brought
-    stress_map = brought[-1]
+    stress_map, panel_spans = brought
     rim = from_behind(rim, "circ", -1)
     order, *kept, first_pairs = pl.pallas_call(
         local_kernel,
@@ -436,9 +431,20 @@
             pltpu.VMEM((2 * ROWS, LANES), f32),
             pltpu.VMEM((2 * ROWS, LANES), i32),
             pltpu.VMEM((3, 3, 8 * PAD, OWN), f32),
+            pltpu.VMEM((3, 8 * PAD, OWN), f32),
         ],
         compiler_params=small,
-    )(own, own_adjoint, *brought)
+    )(
+        held,
+        held_adjoint,
+        node_slot.reshape(ROWS, LANES),
+        thickness,
+        weld_land,
+        membrane,
+        bending,
+        geometric,
+        stress_map,
+    )
     sent, second_pairs = pl.pallas_call(
         rim_kernel,
         out_shape=(shape(GROUPS, PAD, WINDOW), shape(2 * PAD, OWN)),

time: 26.9 us -> 26.7 us (level)
  no operation moved by 1% of the time
where the time goes in v3:
time: 26.7 us; the launch traced here: 26.4 us
  starting transfers between devices  13.9 us (52%)
  waiting for transfers between devices  6.08 us (23%)
  Pallas kernels  4.99 us (19%)
  between operations  1.4 us (5%)
    all_to_all x1, starting transfers between devices, on_device(): received = lax.all_to_all(sent, 'mer', 0, 0)  8.19 us
    ppermute x2, starting transfers between devices, from_behind(): lax.ppermute(block, axis, [((i - distance) % size, i) for i in range(size)])  5.73 us
    ppermute x2, waiting for transfers between devices, from_behind(): lax.ppermute(block, axis, [((i - distance) % size, i) for i in range(size)])  4.84 us
    pallas_call x1, Pallas kernels, on_device(): pl.pallas_call(rim_kernel, out_shape=(shape(GROUPS, PAD, WINDOW), shape(2...  1.37 us
    all_to_all x1, waiting for transfers between devices, on_device(): received = lax.all_to_all(sent, 'mer', 0, 0)  1.24 us
    pallas_call x1, Pallas kernels, on_device(): pl.pallas_call(local_kernel, out_shape=(shape(3, OWN, OWN, dtype=bf16), s...  1.17 us
    pallas_call x1, Pallas kernels, on_device(): pl.pallas_call(gather_kernel, out_shape=(shape(3, 3, DOF, 2, OWN), shape(...  0.91 us
    pallas_call x1, Pallas kernels, on_device(): pl.pallas_call(span_kernel, out_shape=(shape(DOF, 2, OWN), shape(2, MOST)...  0.87 us
  transfers between devices with their start and end apart: 3, of which 3 were waited for; matrix products, arithmetic and copies ran while one was open for 0% of the time, Pallas kernels for 7%

profile of v3, /device:TPU:1, one launch (start us, length us, event | category | flops | bytes accessed | tf_op | source)
XLA Modules:
  0.0 26.4 jit_solution(6820279087368630955)
XLA Ops:
  0.6 0.0 copy-start.1
  0.6 0.0 copy-start.2
  0.7 0.0 copy-start
  0.7 0.0 copy-start.3
  0.7 0.0 copy-start.4
  0.7 0.0 copy-start.5
  0.7 0.9 %shard_map.122 = (f32[3,3,6,2,256]{4,3,2,1,0:T(2,128)S(1)}, f32[6,2,256]{2,1,0:T(2,128)S(1)}, f32[64,256]{1,0:T(8,128)S(1)}, f32[3,24]{1,0:T(4,128)S(1)}, s32[1,16]{1,0:T(1,128)S(1)}) custom-call(f32[3,6,2,4096]{3,2,1,0:T(2,128)} %modes.1, f32[6,2,256]{2,1,0:T(2,128)} %adjoint.1, f32[3,24]{1,0:T(4,128)} %rest_0_.1, s32[1,16]{1,0:T(1,128)} %rest_1_.1), custom_call_target="tpu_custom_call" | custom-call | tf_op jit(solution)/shard_map/pallas_call | solution.py:406
  1.6 5.7 %collective-permute-start = (f32[64,256]{1,0:T(8,128)S(1)}, f32[64,256]{1,0:T(8,128)S(1)}, u32[]{:S(2)}, u32[]{:S(2)}) collective-permute-start(f32[64,256]{1,0:T(8,128)S(1)} %get-tuple-element.23), channel_id=1, source_target_pairs={{16,0},{32,16},{48,32},{64,48},{80,64},{96,80},{112,96},{0,112},{1... | collective-permute-start | bytes 196616 | tf_op jit(solution)/shard_map/ppermute | solution.py:389
  7.3 0.0 copy-done.1
  7.3 0.0 copy-done.2
  7.3 0.0 copy-done
  7.3 0.0 copy-done.3
  7.3 0.0 copy-done.4
  7.3 0.0 copy-done.5
  7.3 1.2 %shard_map.123 = (bf16[3,256,256]{2,1,0:T(8,128)(2,1)S(1)}, f32[3,3,24,256]{3,2,1,0:T(8,128)S(1)}, f32[8,256]{1,0:T(8,128)S(1)}, bf16[176,192]{1,0:T(8,128)(2,1)...) custom-call(f32[3,3,6,2,256]{4,3,2,1,0:T(2,128)S(1)} %get-tuple-element.24.held, ...), custom_call_target="tpu_custom_call" | custom-call | tf_op jit(solution)/shard_map/pallas_call | solution.py:417
  8.5 0.1 collective-permute-done.rim
  8.6 1.4 %shard_map.124 = (f32[16,8,128]{2,1,0:T(8,128)}, f32[16,256]{1,0:T(8,128)S(1)}) custom-call(f32[64,256]{1,0:T(8,128)S(1)} %collective-permute-done.rim, bf16[3,256,256]{2,1,0:T(8,128)(2,1)S(1)} %get-tuple-element.27.order, f32[3,3,24,256]{3,2,1,0:T(8,128)S(1)} %get-tuple-element.28.second, f32[8,256]{1,0:T(8,128)S(1)} %get-tuple-element.29.second_adjoint, ...), custom_call_target="tpu_custom_call" | custom-call | tf_op jit(solution)/shard_map/pallas_call | solution.py:448
  10.0 8.2 %all-to-all-start = ((f32[16,8,128]{2,1,0:T(8,128)}), f32[16,8,128]{2,1,0:T(8,128)S(1)}, u32[]{:S(2)}, u32[]{:S(2)}) async-start(f32[16,8,128]{2,1,0:T(8,128)} %get-tuple-element.34), calls=%async_computation | async-start | bytes 131072 | tf_op jit(solution)/shard_map/all_to_all | solution.py:460
  18.8 0.5 %shard_map.125 = (f32[16,256]{1,0:T(8,128)S(1)}, f32[8,256]{1,0:T(8,128)S(1)}) custom-call(f32[16,256]{1,0:T(8,128)S(1)} %get-tuple-element.35.first_pairs, f32[16,256]{1,0:T(8,128)S(1)} %get-tuple-element.37.second_pairs, bf16[3,256,256]{2,1,0:T(8,128)(2,1)S(1)} %get-tuple-element.27.order, f32[3,24]{1,0:T(4,128)S(1)} %get-tuple-element.26.stress_map, ...), custom_call_target="tpu_custom_call" | custom-call | tf_op jit(solution)/shard_map/pallas_call | solution.py:462
  19.3 0.1 collective-permute-start.1
  19.4 0.2 shard_map.126
  19.6 4.7 %collective-permute-done.1.carry = f32[8,256]{1,0:T(8,128)S(1)} collective-permute-done((f32[8,256]{1,0:T(8,128)S(1)}, f32[8,256]{1,0:T(8,128)S(1)}, u32[]{:S(2)}, u32[]{:S(2)}) %collective-permute-start.1) | collective-permute-done | bytes 8224 | tf_op jit(solution)/shard_map/ppermute | solution.py:389
  24.3 1.2 %all-to-all-done.received = f32[16,8,128]{2,1,0:T(8,128)S(1)} async-done(((f32[16,8,128]{2,1,0:T(8,128)}), f32[16,8,128]{2,1,0:T(8,128)S(1)}, u32[]{:S(2)}, u32[]{:S(2)}) %all-to-all-start) | async-done | bytes 65568 | tf_op jit(solution)/shard_map/all_to_all | solution.py:460
  25.5 0.9 %shard_map.127 = (f32[6,2,256]{2,1,0:T(2,128)}, f32[2,768]{1,0:T(2,128)}) custom-call(f32[16,8,128]{2,1,0:T(8,128)S(1)} %all-to-all-done.received, f32[16,256]{1,0:T(8,128)S(1)} %get-tuple-element.39.loads, f32[8,256]{1,0:T(8,128)S(1)} %collective-permute-done.1.carry, bf16[192,768]{1,0:T(8,128)(2,1)S(1)} %get-tuple-element.41.spread_now, ...), custom_call_target="tpu_custom_call" | custom-call | tf_op jit(solution)/shard_map/pallas_call | solution.py:477
Async XLA Ops:
  0.6 6.6 %copy-start.1 = (f32[2,4096]{1,0:T(2,128)S(1)}, f32[2,4096]{1,0:T(2,128)}, u32[]{:S(2)}) copy-start(f32[2,4096]{1,0:T(2,128)} %thickness.1) | copy-start | bytes 98308
  0.6 6.6 %copy-start.2 = (s32[2,4096]{1,0:T(2,128)S(1)}, s32[2,4096]{1,0:T(2,128)}, u32[]{:S(2)}) copy-start(s32[2,4096]{1,0:T(2,128)} %weld.1) | copy-start | bytes 98308
  0.7 6.6 %copy-start = (f32[3,24,24]{2,1,0:T(8,128)S(1)}, f32[3,24,24]{2,1,0:T(8,128)}, u32[]{:S(2)}) copy-start(f32[3,24,24]{2,1,0:T(8,128)} %geometric.1) | copy-start | bytes 20740
  0.7 6.6 %copy-start.3 = (s32[4096]{0:T(1024)S(1)}, s32[4096]{0:T(1024)}, u32[]{:S(2)}) copy-start(s32[4096]{0:T(1024)} %param.13) | copy-start | bytes 49156
  0.7 6.6 %copy-start.4 = (f32[24,24]{1,0:T(8,128)S(1)}, f32[24,24]{1,0:T(8,128)}, u32[]{:S(2)}) copy-start(f32[24,24]{1,0:T(8,128)} %membrane.1) | copy-start | bytes 6916
  0.7 6.6 %copy-start.5 = (f32[24,24]{1,0:T(8,128)S(1)}, f32[24,24]{1,0:T(8,128)}, u32[]{:S(2)}) copy-start(f32[24,24]{1,0:T(8,128)} %bending.1) | copy-start | bytes 6916
  1.6 7.0 %collective-permute-start = (f32[64,256]{1,0:T(8,128)S(1)}, f32[64,256]{1,0:T(8,128)S(1)}, u32[]{:S(2)}, u32[]{:S(2)}) collective-permute-start(f32[64,256]{1,0:T(8,128)S(1)} %get-tuple-element.23), channel_id=1, source_target_pairs={{16,0},{32,16},{48,32},{64,48},{80,64},{96,80},{112,96},{0,112},{1... | collective-permute-start | bytes 196616 | tf_op jit(solution)/shard_map/ppermute | solution.py:389
  10.0 15.6 %all-to-all-start = ((f32[16,8,128]{2,1,0:T(8,128)}), f32[16,8,128]{2,1,0:T(8,128)S(1)}, u32[]{:S(2)}, u32[]{:S(2)}) async-start(f32[16,8,128]{2,1,0:T(8,128)} %get-tuple-element.34), calls=%async_computation | async-start | bytes 131072 | tf_op jit(solution)/shard_map/all_to_all | solution.py:460
  19.3 5.0 %collective-permute-start.1 = (f32[8,256]{1,0:T(8,128)S(1)}, f32[8,256]{1,0:T(8,128)S(1)}, u32[]{:S(2)}, u32[]{:S(2)}) collective-permute-start(f32[8,256]{1,0:T(8,128)S(1)} %get-tuple-element.40), channel_id=1, source_target_pairs={{112,0},{0,16},{16,32},{32,48},{48,64},{64,80},{80,96},{96,112},{1... | collective-permute-start | bytes 24584 | tf_op jit(solution)/shard_map/ppermute | solution.py:389

commit v4 on v3

--- a/solution.py
+++ b/solution.py
@@ -21,6 +21,7 @@
 f32, bf16, i32 = jnp.float32, jnp.bfloat16, jnp.int32
 vmem = pl.BlockSpec(memory_space=pltpu.VMEM)
 smem = pl.BlockSpec(memory_space=pltpu.SMEM)
+raw = pl.BlockSpec(memory_space=pl.ANY)
 hbm = pl.BlockSpec(memory_space=pltpu.HBM)
 small = pltpu.CompilerParams(vmem_limit_bytes=12 << 20)
 
@@ -91,40 +92,55 @@
     return jnp.sum(x, axis=0, keepdims=True)
 
 
+def pair_terms(corner_parts, d, weights):
+    pairs = [jnp.zeros((PAD, OWN), f32)] * 3
+    products = []
+    for f in range(2):
+        three = corner_parts(f, d)
+        value = (three[0] + three[1]) + three[2]
+        product = matmul(weights, right_stack([t.astype(bf16) for t in three], 0))
+        products.append((value, product))
+        first = product.shape[0] - 96
+        pairs = [
+            pairs[s] + fold(value * product[first + 32 * s : first + 32 * s + 32]) for s in range(3)
+        ]
+    return [column_sum(x) for x in pairs], products
+
+
 def cycle_terms(corner_parts, adjoint, growth, thick, weights):
     bend = [3.0 * t * t for t in thick]
-    pair_weights = weights[64:160]
+    pairs, products = pair_terms(corner_parts, 1, weights[0:160])
+    stiff = jnp.zeros((PAD, OWN), f32)
+    for value, product in products:
+        stiff = stiff + fold(value * (product[0:32] + bend[1] * product[32:64]))
     prestate_weights = jnp.concatenate([weights[0:64], weights[160:176]], axis=0)
-    outcome = {}
-    for d in (1, 0):
-        stiff = jnp.zeros((PAD, OWN), f32)
-        pairs = [jnp.zeros((PAD, OWN), f32)] * 3
-        for f in range(2):
-            three = corner_parts(f, d)
-            value = (three[0] + three[1]) + three[2]
-            stack = right_stack([t.astype(bf16) for t in three], 0)
-            if d == 1:
-                product = matmul(weights[0:160], stack)
-                stiff = stiff + fold(value * (product[0:32] + bend[d] * product[32:64]))
-                product = product[64:160]
-            else:
-                product = matmul(pair_weights, stack)
-            pairs = [pairs[s] + fold(value * product[32 * s : 32 * s + 32]) for s in range(3)]
-        pairs = [column_sum(x) for x in pairs]
-        stack = right_stack([t.astype(bf16) for t in corner_parts(2, d)], 0)
-        product = matmul(prestate_weights, stack)
-        tangent = product[0:32] + bend[d] * product[32:64]
-        if d == 1:
-            aterm = column_sum(adjoint[0] * tangent[0:8] + adjoint[1] * tangent[8:16])
-            coupling = (
-                product[64:65] * pairs[0] + product[65:66] * pairs[1]
-            ) + product[66:67] * pairs[2]
-            rows = [growth[d] * (column_sum(stiff) - aterm), growth[d] * coupling]
-        else:
-            aterm = column_sum(adjoint[0] * tangent[24:32] + adjoint[1] * tangent[16:24])
-            rows.append(-(growth[d] * aterm))
-        outcome[d] = [thick[d] * x for x in pairs] + [jnp.zeros((5, OWN), f32)]
-    return rows, jnp.concatenate(outcome[0] + outcome[1], axis=0)
+    here, before = [
+        matmul(prestate_weights, right_stack([t.astype(bf16) for t in corner_parts(2, d)], 0))
+        for d in (1, 0)
+    ]
+    tangent = here[0:16] + bend[1] * here[32:48]
+    aterm = column_sum(adjoint[0] * tangent[0:8] + adjoint[1] * tangent[8:16])
+    coupling = (here[64:65] * pairs[0] + here[65:66] * pairs[1]) + here[66:67] * pairs[2]
+    tangent = before[16:32] + bend[0] * before[48:64]
+    late_aterm = column_sum(adjoint[0] * tangent[8:16] + adjoint[1] * tangent[0:8])
+    rows = [
+        growth[1] * (column_sum(stiff) - aterm),
+        growth[1] * coupling,
+        -(growth[0] * late_aterm),
+    ]
+    return rows, pairs
+
+
+def pair_rows(before, here, thick):
+    return jnp.concatenate(
+        [
+            *[thick[0] * x for x in before],
+            jnp.zeros((5, OWN), f32),
+            *[thick[1] * x for x in here],
+            jnp.zeros((5, OWN), f32),
+        ],
+        axis=0,
+    )
 
 
 def corner_rows():
@@ -246,15 +262,13 @@
         for g in (48, 56)
     ]
     second_adjoint[...] = adjoint[1]
-    rows, pair_rows = cycle_terms(
-        corner_parts,
-        adjoint,
-        [growth[d, 0] for d in range(2)],
-        [thick[d, 0] for d in range(2)],
-        weights[...],
+    thick = [thick[d, 0] for d in range(2)]
+    rows, here = cycle_terms(
+        corner_parts, adjoint, [growth[d, 0] for d in range(2)], thick, weights[...]
     )
     gradients[...] = jnp.concatenate(rows + [jnp.zeros((5, OWN), f32)], axis=0)
-    pairs[...] = pair_rows
+    before, _ = pair_terms(corner_parts, 0, weights[64:160, :])
+    pairs[...] = pair_rows(before, here, thick)
 
 
 def rim_kernel(
@@ -270,7 +284,9 @@
     pairs,
     nodes,
     counts,
+    windows,
     sem,
+    store_sem,
 ):
     fetch = pltpu.make_async_copy(spans, counts, sem)
     fetch.start()
@@ -298,14 +314,10 @@
         ]
 
     adjoint = [second_adjoint[...], (nodes[1, 0, 24:32, :] + nodes[1, 1, 24:32, :]) + nodes[1, 2, 24:32, :]]
-    rows, pair_rows = cycle_terms(
-        corner_parts,
-        adjoint,
-        [scalings[0:1, :], scalings[1:2, :]],
-        [scalings[2:3, :], scalings[3:4, :]],
-        weights[...],
+    thick = [scalings[2:3, :], scalings[3:4, :]]
+    rows, here = cycle_terms(
+        corner_parts, adjoint, [scalings[0:1, :], scalings[1:2, :]], thick, weights[...]
     )
-    pairs[...] = pair_rows
 
     odd = (lax.axis_index("mer") & 1) == 1
     none = jnp.zeros((1, OWN), f32)
@@ -324,8 +336,13 @@
         first = (start >> 4) & (OWN - 1)
         turned = pltpu.roll(now, (OWN - first) & (OWN - 1), 1)
         turned_late = pltpu.roll(late, (OWN + HALF - first) & (OWN - 1), 1)
-        sent[target] = jnp.where(lower, turned[:, 0:WINDOW], turned_late[:, 0:WINDOW])
+        windows[target] = jnp.where(lower, turned[:, 0:WINDOW], turned_late[:, 0:WINDOW])
         start = start + counts[0, target]
+    store = pltpu.make_async_copy(windows, sent, store_sem)
+    store.start()
+    before, _ = pair_terms(corner_parts, 0, weights[64:160, :])
+    pairs[...] = pair_rows(before, here, thick)
+    store.wait()
 
 
 def load_kernel(first_pairs, second_pairs, order, stress_map, factor, loads, carry):
@@ -449,10 +466,12 @@
         rim_kernel,
         out_shape=(shape(GROUPS, PAD, WINDOW), shape(2 * PAD, OWN)),
         in_specs=[vmem] * 8,
-        out_specs=(vmem,) * 2,
+        out_specs=(raw, vmem),
         scratch_shapes=[
             pltpu.VMEM((3, 3, 4 * PAD, OWN), f32),
             pltpu.SMEM((1, GROUPS), i32),
+            pltpu.VMEM((GROUPS, PAD, WINDOW), f32),
+            pltpu.SemaphoreType.DMA,
             pltpu.SemaphoreType.DMA,
         ],
         compiler_params=small,

time: 26.7 us -> 26.6 us (level)
  no operation moved by 1% of the time
where the time goes in v4:
time: 26.6 us; the launch traced here: 26.4 us
  starting transfers between devices  13.9 us (52%)
  waiting for transfers between devices  6.08 us (23%)
  Pallas kernels  4.96 us (19%)
  between operations  1.4 us (5%)
    all_to_all x1, starting transfers between devices, on_device(): received = lax.all_to_all(sent, 'mer', 0, 0)  8.19 us
    ppermute x2, starting transfers between devices, from_behind(): lax.ppermute(block, axis, [((i - distance) % size, i) for i in range(size)])  5.73 us
    ppermute x2, waiting for transfers between devices, from_behind(): lax.ppermute(block, axis, [((i - distance) % size, i) for i in range(size)])  4.83 us
    pallas_call x1, Pallas kernels, on_device(): pl.pallas_call(rim_kernel, out_shape=(shape(GROUPS, PAD, WINDOW), shape(2...  1.34 us
    all_to_all x1, waiting for transfers between devices, on_device(): received = lax.all_to_all(sent, 'mer', 0, 0)  1.24 us
    pallas_call x1, Pallas kernels, on_device(): pl.pallas_call(local_kernel, out_shape=(shape(3, OWN, OWN, dtype=bf16), s...  1.17 us
    pallas_call x1, Pallas kernels, on_device(): pl.pallas_call(gather_kernel, out_shape=(shape(3, 3, DOF, 2, OWN), shape(...  0.91 us
    pallas_call x1, Pallas kernels, on_device(): pl.pallas_call(span_kernel, out_shape=(shape(DOF, 2, OWN), shape(2, MOST)...  0.87 us
  transfers between devices with their start and end apart: 3, of which 3 were waited for; matrix products, arithmetic and copies ran while one was open for 0% of the time, Pallas kernels for 7%

profile of v4, /device:TPU:1, one launch (start us, length us, event | category | flops | bytes accessed | tf_op | source)
XLA Modules:
  0.0 26.4 jit_solution(8486601147335529920)
XLA Ops:
  0.6 0.0 copy-start.1
  0.6 0.0 copy-start.2
  0.7 0.0 copy-start
  0.7 0.0 copy-start.3
  0.7 0.0 copy-start.4
  0.7 0.0 copy-start.5
  0.7 0.9 %shard_map.122 = (f32[3,3,6,2,256]{4,3,2,1,0:T(2,128)S(1)}, f32[6,2,256]{2,1,0:T(2,128)S(1)}, f32[64,256]{1,0:T(8,128)S(1)}, f32[3,24]{1,0:T(4,128)S(1)}, s32[1,16]{1,0:T(1,128)S(1)}) custom-call(f32[3,6,2,4096]{3,2,1,0:T(2,128)} %modes.1, f32[6,2,256]{2,1,0:T(2,128)} %adjoint.1, f32[3,24]{1,0:T(4,128)} %rest_0_.1, s32[1,16]{1,0:T(1,128)} %rest_1_.1), custom_call_target="tpu_custom_call" | custom-call | tf_op jit(solution)/shard_map/pallas_call | solution.py:423
  1.6 5.7 %collective-permute-start = (f32[64,256]{1,0:T(8,128)S(1)}, f32[64,256]{1,0:T(8,128)S(1)}, u32[]{:S(2)}, u32[]{:S(2)}) collective-permute-start(f32[64,256]{1,0:T(8,128)S(1)} %get-tuple-element.23), channel_id=1, source_target_pairs={{16,0},{32,16},{48,32},{64,48},{80,64},{96,80},{112,96},{0,112},{1... | collective-permute-start | bytes 196616 | tf_op jit(solution)/shard_map/ppermute | solution.py:406
  7.3 0.0 copy-done.1
  7.3 0.0 copy-done.2
  7.3 0.0 copy-done
  7.3 0.0 copy-done.3
  7.3 0.0 copy-done.4
  7.3 0.0 copy-done.5
  7.3 1.2 %shard_map.123 = (bf16[3,256,256]{2,1,0:T(8,128)(2,1)S(1)}, f32[3,3,24,256]{3,2,1,0:T(8,128)S(1)}, f32[8,256]{1,0:T(8,128)S(1)}, bf16[176,192]{1,0:T(8,128)(2,1)...) custom-call(f32[3,3,6,2,256]{4,3,2,1,0:T(2,128)S(1)} %get-tuple-element.24.held, ...), custom_call_target="tpu_custom_call" | custom-call | tf_op jit(solution)/shard_map/pallas_call | solution.py:434
  8.5 0.1 collective-permute-done.rim
  8.6 1.3 %shard_map.124 = (f32[16,8,128]{2,1,0:T(8,128)}, f32[16,256]{1,0:T(8,128)S(1)}) custom-call(f32[64,256]{1,0:T(8,128)S(1)} %collective-permute-done.rim, bf16[3,256,256]{2,1,0:T(8,128)(2,1)S(1)} %get-tuple-element.27.order, f32[3,3,24,256]{3,2,1,0:T(8,128)S(1)} %get-tuple-element.28.second, f32[8,256]{1,0:T(8,128)S(1)} %get-tuple-element.29.second_adjoint, ...), custom_call_target="tpu_custom_call" | custom-call | tf_op jit(solution)/shard_map/pallas_call | solution.py:465
  10.0 8.2 %all-to-all-start = ((f32[16,8,128]{2,1,0:T(8,128)}), f32[16,8,128]{2,1,0:T(8,128)S(1)}, u32[]{:S(2)}, u32[]{:S(2)}) async-start(f32[16,8,128]{2,1,0:T(8,128)} %get-tuple-element.34), calls=%async_computation | async-start | bytes 131072 | tf_op jit(solution)/shard_map/all_to_all | solution.py:479
  18.8 0.5 %shard_map.125 = (f32[16,256]{1,0:T(8,128)S(1)}, f32[8,256]{1,0:T(8,128)S(1)}) custom-call(f32[16,256]{1,0:T(8,128)S(1)} %get-tuple-element.35.first_pairs, f32[16,256]{1,0:T(8,128)S(1)} %get-tuple-element.37.second_pairs, bf16[3,256,256]{2,1,0:T(8,128)(2,1)S(1)} %get-tuple-element.27.order, f32[3,24]{1,0:T(4,128)S(1)} %get-tuple-element.26.stress_map, ...), custom_call_target="tpu_custom_call" | custom-call | tf_op jit(solution)/shard_map/pallas_call | solution.py:481
  19.3 0.1 collective-permute-start.1
  19.4 0.2 shard_map.126
  19.6 4.7 %collective-permute-done.1.carry = f32[8,256]{1,0:T(8,128)S(1)} collective-permute-done((f32[8,256]{1,0:T(8,128)S(1)}, f32[8,256]{1,0:T(8,128)S(1)}, u32[]{:S(2)}, u32[]{:S(2)}) %collective-permute-start.1) | collective-permute-done | bytes 8224 | tf_op jit(solution)/shard_map/ppermute | solution.py:406
  24.3 1.2 %all-to-all-done.received = f32[16,8,128]{2,1,0:T(8,128)S(1)} async-done(((f32[16,8,128]{2,1,0:T(8,128)}), f32[16,8,128]{2,1,0:T(8,128)S(1)}, u32[]{:S(2)}, u32[]{:S(2)}) %all-to-all-start) | async-done | bytes 65568 | tf_op jit(solution)/shard_map/all_to_all | solution.py:479
  25.5 0.9 %shard_map.127 = (f32[6,2,256]{2,1,0:T(2,128)}, f32[2,768]{1,0:T(2,128)}) custom-call(f32[16,8,128]{2,1,0:T(8,128)S(1)} %all-to-all-done.received, f32[16,256]{1,0:T(8,128)S(1)} %get-tuple-element.39.loads, f32[8,256]{1,0:T(8,128)S(1)} %collective-permute-done.1.carry, bf16[192,768]{1,0:T(8,128)(2,1)S(1)} %get-tuple-element.41.spread_now, ...), custom_call_target="tpu_custom_call" | custom-call | tf_op jit(solution)/shard_map/pallas_call | solution.py:496
Async XLA Ops:
  0.6 6.6 %copy-start.1 = (f32[2,4096]{1,0:T(2,128)S(1)}, f32[2,4096]{1,0:T(2,128)}, u32[]{:S(2)}) copy-start(f32[2,4096]{1,0:T(2,128)} %thickness.1) | copy-start | bytes 98308
  0.6 6.6 %copy-start.2 = (s32[2,4096]{1,0:T(2,128)S(1)}, s32[2,4096]{1,0:T(2,128)}, u32[]{:S(2)}) copy-start(s32[2,4096]{1,0:T(2,128)} %weld.1) | copy-start | bytes 98308
  0.7 6.6 %copy-start = (f32[3,24,24]{2,1,0:T(8,128)S(1)}, f32[3,24,24]{2,1,0:T(8,128)}, u32[]{:S(2)}) copy-start(f32[3,24,24]{2,1,0:T(8,128)} %geometric.1) | copy-start | bytes 20740
  0.7 6.6 %copy-start.3 = (s32[4096]{0:T(1024)S(1)}, s32[4096]{0:T(1024)}, u32[]{:S(2)}) copy-start(s32[4096]{0:T(1024)} %param.13) | copy-start | bytes 49156
  0.7 6.6 %copy-start.4 = (f32[24,24]{1,0:T(8,128)S(1)}, f32[24,24]{1,0:T(8,128)}, u32[]{:S(2)}) copy-start(f32[24,24]{1,0:T(8,128)} %membrane.1) | copy-start | bytes 6916
  0.7 6.6 %copy-start.5 = (f32[24,24]{1,0:T(8,128)S(1)}, f32[24,24]{1,0:T(8,128)}, u32[]{:S(2)}) copy-start(f32[24,24]{1,0:T(8,128)} %bending.1) | copy-start | bytes 6916
  1.6 7.0 %collective-permute-start = (f32[64,256]{1,0:T(8,128)S(1)}, f32[64,256]{1,0:T(8,128)S(1)}, u32[]{:S(2)}, u32[]{:S(2)}) collective-permute-start(f32[64,256]{1,0:T(8,128)S(1)} %get-tuple-element.23), channel_id=1, source_target_pairs={{16,0},{32,16},{48,32},{64,48},{80,64},{96,80},{112,96},{0,112},{1... | collective-permute-start | bytes 196616 | tf_op jit(solution)/shard_map/ppermute | solution.py:406
  10.0 15.6 %all-to-all-start = ((f32[16,8,128]{2,1,0:T(8,128)}), f32[16,8,128]{2,1,0:T(8,128)S(1)}, u32[]{:S(2)}, u32[]{:S(2)}) async-start(f32[16,8,128]{2,1,0:T(8,128)} %get-tuple-element.34), calls=%async_computation | async-start | bytes 131072 | tf_op jit(solution)/shard_map/all_to_all | solution.py:479
  19.3 5.0 %collective-permute-start.1 = (f32[8,256]{1,0:T(8,128)S(1)}, f32[8,256]{1,0:T(8,128)S(1)}, u32[]{:S(2)}, u32[]{:S(2)}) collective-permute-start(f32[8,256]{1,0:T(8,128)S(1)} %get-tuple-element.40), channel_id=1, source_target_pairs={{112,0},{0,16},{16,32},{32,48},{48,64},{64,80},{80,96},{96,112},{1... | collective-permute-start | bytes 24584 | tf_op jit(solution)/shard_map/ppermute | solution.py:406
